TPU v7x, 512 devices: a whole 4x4x16 slice. The times are simulated.
512 devices in a mesh: head: 4 (over y), tok: 128 (over z, x, core).
Axes of the slice: x: 4, y: 4, z: 16, core: 2. Of those that a mesh axis runs over, the one named last changes fastest.
Arguments:
- query_input: bfloat16 [32768, 2048], P('tok', 'head'), may hold values from -6 to 6
- key_input: bfloat16 [32768, 2048], P('tok', 'head'), may hold values from -6 to 6
- value_input: bfloat16 [32768, 2048], P('tok', 'head'), may hold values from -6 to 6
- out_grad: bfloat16 [32768, 2048], P('tok', 'head'), may hold values from -0.4453125 to 0.4453125
- token_rates: float32 [32768, 4], P('tok', 'head'), may hold values from 0.00022097086 to 0.0022097088
- out_gain: float32 [2048], P('head'), may hold values from 0.1 to 1.9
- gate_prior: bfloat16 [4, 512, 256], P('head'), may hold values from -0.8242256 to 0.8242256
- up_prior: bfloat16 [4, 512, 256], P('head'), may hold values from -0.8242256 to 0.8242256
- down_prior: bfloat16 [4, 256, 512], P('head'), may hold values from -3.496893 to 3.496893
Outputs:
- query_grad: bfloat16 [32768, 2048], P('tok', 'head')
- key_grad: bfloat16 [32768, 2048], P('tok', 'head')
- value_grad: bfloat16 [32768, 2048], P('tok', 'head')
- gate_prior_grad: float32 [4, 512, 256], P('head', None, 'tok')
- up_prior_grad: float32 [4, 512, 256], P('head', None, 'tok')
- down_prior_grad: float32 [4, 256, 512], P('head', None, 'tok')
All inputs are finite; a program needn't handle non-finite values.
Results may differ from a plain program's by a relative error of at most 0.014.
Values may be sent and summed in bfloat16 or wider, within the bound.
A program may use at most 64 MiB of HBM per device.

v0:
```python
import jax
import jax.numpy as jnp
from jax import lax
from jax.sharding import PartitionSpec as P

EPSILON = 1e-06


def matmul(first_op, second_op):
    return jnp.dot(first_op, second_op, preferred_element_type=jnp.float32)


def contract_rows(first_op, second_op):
    return lax.dot_general(
        first_op, second_op, (((0,), (0,)), ((), ())), preferred_element_type=jnp.float32
    )


def contract_cols(first_op, second_op):
    return lax.dot_general(
        first_op, second_op, (((1,), (1,)), ((), ())), preferred_element_type=jnp.float32
    )


def silu_parts(hidden):
    sigmoid_value = jax.nn.sigmoid(hidden)
    silu_value = hidden * sigmoid_value
    silu_slope = sigmoid_value * (1.0 + hidden * (1.0 - sigmoid_value))
    curvature = sigmoid_value * (1.0 - sigmoid_value) * (2.0 + hidden * (1.0 - 2.0 * sigmoid_value))
    return (silu_value, silu_slope, curvature)


def update_forward(key_head, value_head, rate_head, priors):
    gate_weight, up_weight, down_weight = priors
    gate_pre = matmul(key_head, gate_weight)
    up_pre = matmul(key_head, up_weight)
    silu_value, silu_slope, curvature = silu_parts(gate_pre)
    mixed_act = (silu_value * up_pre).astype(jnp.bfloat16)
    value_push = (-rate_head[:, None] * value_head.astype(jnp.float32)).astype(jnp.bfloat16)
    down_update = contract_rows(mixed_act, value_push)
    down_back = contract_cols(value_push, down_weight)
    gate_back = (down_back * up_pre * silu_slope).astype(jnp.bfloat16)
    up_back = (down_back * silu_value).astype(jnp.bfloat16)
    gate_update = contract_rows(key_head, gate_back)
    up_update = contract_rows(key_head, up_back)
    update_saved = (
        up_pre,
        silu_value,
        silu_slope,
        curvature,
        mixed_act,
        value_push,
        down_back,
        gate_back,
        up_back,
    )
    return ((gate_update, up_update, down_update), update_saved)


def renormalize(prior, update):
    prior_f = prior.astype(jnp.float32)
    moved_weight = prior_f - update
    prior_norm = jnp.sqrt(jnp.sum(prior_f * prior_f, axis=0) + EPSILON)
    moved_norm = jnp.sqrt(jnp.sum(moved_weight * moved_weight, axis=0) + EPSILON)
    return (moved_weight, prior_norm, moved_norm)


def apply_forward(query_head, fast_weights):
    gate_pre = matmul(query_head, fast_weights[0])
    up_pre = matmul(query_head, fast_weights[1])
    silu_value, silu_slope, curvature = silu_parts(gate_pre)
    mixed_act = (silu_value * up_pre).astype(jnp.bfloat16)
    output = matmul(mixed_act, fast_weights[2])
    return (output, (up_pre, silu_value, silu_slope, mixed_act))


def apply_backward(query_head, fast_weights, apply_saved, out_back):
    up_pre, silu_value, silu_slope, mixed_act = apply_saved
    down_grad = contract_rows(mixed_act, out_back)
    mixed_back = contract_cols(out_back, fast_weights[2])
    gate_back = (mixed_back * up_pre * silu_slope).astype(jnp.bfloat16)
    up_back = (mixed_back * silu_value).astype(jnp.bfloat16)
    gate_grad = contract_rows(query_head, gate_back)
    up_grad = contract_rows(query_head, up_back)
    query_back = (
        contract_cols(gate_back, fast_weights[0]) + contract_cols(up_back, fast_weights[1])
    ).astype(jnp.bfloat16)
    return ((gate_grad, up_grad, down_grad), query_back)


def norm_adjoint(prior, moved_weight, prior_norm, moved_norm, fast_grad, column_dot):
    moved_grad = (
        prior_norm
        / moved_norm
        * (fast_grad - moved_weight * (column_dot / (moved_norm * moved_norm)))
    )
    direct = prior.astype(jnp.float32) * (column_dot / (moved_norm * prior_norm))
    return (moved_grad, direct)


def second_adjoint(key_head, rate_head, priors, update_saved, cotangent):
    gate_weight, up_weight, down_weight = priors
    (
        up_pre,
        silu_value,
        silu_slope,
        curvature,
        mixed_act,
        value_push,
        down_back,
        gate_back,
        up_back,
    ) = update_saved
    gate_cot, up_cot, down_cot = cotangent
    gate_bar = matmul(key_head, gate_cot)
    up_bar = matmul(key_head, up_cot)
    mixed_bar = contract_cols(value_push, down_cot)
    push_bar = matmul(mixed_act, down_cot)
    down_back_bar = (gate_bar * up_pre * silu_slope + up_bar * silu_value).astype(jnp.bfloat16)
    up_pre_bar = (gate_bar * down_back * silu_slope + mixed_bar * silu_value).astype(jnp.bfloat16)
    gate_pre_bar = (
        (up_bar * down_back + mixed_bar * up_pre) * silu_slope
        + gate_bar * down_back * up_pre * curvature
    ).astype(jnp.bfloat16)
    down_prior_bar = contract_rows(down_back_bar, value_push)
    gate_prior_bar = contract_rows(key_head, gate_pre_bar)
    up_prior_bar = contract_rows(key_head, up_pre_bar)
    value_grad = (rate_head[:, None] * (push_bar + matmul(down_back_bar, down_weight))).astype(
        jnp.bfloat16
    )
    key_total = (
        contract_cols(gate_back, gate_cot)
        + contract_cols(up_back, up_cot)
        + contract_cols(gate_pre_bar, gate_weight)
        + contract_cols(up_pre_bar, up_weight)
    )
    key_grad = (-key_total).astype(jnp.bfloat16)
    return ((gate_prior_bar, up_prior_bar, down_prior_bar), key_grad, value_grad)


def per_device(
    query_input,
    key_input,
    value_input,
    out_grad,
    token_rates,
    out_gain,
    gate_prior,
    up_prior,
    down_prior,
):
    rate_head = token_rates[:, 0]
    priors = (gate_prior[0], up_prior[0], down_prior[0])
    tok_count = lax.axis_size("tok")
    tok_index = lax.axis_index("tok")
    local_updates, update_saved = update_forward(key_input, value_input, rate_head, priors)
    update_sums = lax.psum((local_updates[0], local_updates[1], local_updates[2]), "tok")
    renormed = [
        renormalize(priors[matrix_index], update_sums[matrix_index]) for matrix_index in range(3)
    ]
    fast_weights = tuple(
        (
            (moved_weight * (prior_norm / moved_norm)).astype(jnp.bfloat16)
            for moved_weight, prior_norm, moved_norm in renormed
        )
    )
    output, apply_saved = apply_forward(query_input, fast_weights)
    gain_weighted = out_grad.astype(jnp.float32) * out_gain
    square_sum, dot_sum = lax.psum(
        (jnp.sum(output * output, axis=1), jnp.sum(gain_weighted * output, axis=1)), "head"
    )
    full_width = lax.axis_size("head") * output.shape[1]
    inverse = lax.rsqrt(square_sum / full_width + EPSILON)
    out_back = (
        inverse[:, None] * gain_weighted
        - output * (inverse * inverse * inverse * dot_sum / full_width)[:, None]
    ).astype(jnp.bfloat16)
    fast_parts, query_grad = apply_backward(query_input, fast_weights, apply_saved, out_back)
    owned_parts = []
    fast_grads = lax.psum((fast_parts[0], fast_parts[1], fast_parts[2]), "tok")
    pieces = []
    for matrix_index in range(3):
        moved_weight, prior_norm, moved_norm = renormed[matrix_index]
        column_dot = jnp.sum(fast_grads[matrix_index] * moved_weight, axis=0)
        moved_grad, direct = norm_adjoint(
            priors[matrix_index],
            moved_weight,
            prior_norm,
            moved_norm,
            fast_grads[matrix_index],
            column_dot,
        )
        pieces.append(moved_grad.astype(jnp.bfloat16))
        shard_span = moved_weight.shape[1] // tok_count
        owned_parts.append(
            lax.dynamic_slice_in_dim(moved_grad + direct, tok_index * shard_span, shard_span, 1)
        )
    cotangent = (pieces[0], pieces[1], pieces[2])
    prior_bars, key_grad, value_grad = second_adjoint(
        key_input, rate_head, priors, update_saved, cotangent
    )
    prior_terms = [-prior_bars[matrix_index] for matrix_index in range(3)]
    summed_parts = (
        lax.psum_scatter(prior_terms[0], "tok", scatter_dimension=1, tiled=True),
        lax.psum_scatter(prior_terms[1], "tok", scatter_dimension=1, tiled=True),
        lax.psum_scatter(prior_terms[2], "tok", scatter_dimension=1, tiled=True),
    )
    results = tuple(
        (summed_parts[matrix_index] + owned_parts[matrix_index] for matrix_index in range(3))
    )
    return (query_grad, key_grad, value_grad, results[0][None], results[1][None], results[2][None])


def solution(mesh):
    in_specs = (
        P("tok", "head"),
        P("tok", "head"),
        P("tok", "head"),
        P("tok", "head"),
        P("tok", "head"),
        P("head"),
        P("head", None, None),
        P("head", None, None),
        P("head", None, None),
    )
    out_specs = (
        P("tok", "head"),
        P("tok", "head"),
        P("tok", "head"),
        P("head", None, "tok"),
        P("head", None, "tok"),
        P("head", None, "tok"),
    )
    return jax.shard_map(
        per_device, mesh=mesh, in_specs=in_specs, out_specs=out_specs, check_vma=False
    )
```

profile of v0, /device:TPU:1, one launch (start us, length us, event | category | flops | bytes accessed | tf_op | source)
XLA Modules:
  0.0 1111.1 jit_solution(10692967141471436718)
XLA Ops:
  8.1 1.2 fusion.14
  11.4 1.1 convolution_bitcast_fusion.3
  12.4 1.0 convolution_bitcast_fusion.2
  13.5 1.1 fusion.48
  16.7 351.2 %all-reduce.15.cloned.1.call-done = (f32[512,256]{0,1:T(8,128)}, f32[512,256]{0,1:T(8,128)}, f32[256,512]{1,0:T(8,128)}) async-done(((f32[512,256]{0,1:T(8,128)}, f32[512,256]{0,1:T(8,128)}, f32[256,512]{1,0:T(8,128)}), (f32[512,256]{0,1:T(8,128)}, f32[512,256]{0,1:T(8,128)}, f32[256,512]{1,0:T(8,128)})) %all-reduce.15.cloned.1.call-update) | async-done | bytes 1572880 | tf_op jit(solution)/shard_map/psum | solution.py:157
  367.9 1.3 multiply_reduce_fusion.9
  373.9 1.0 multiply_convert_fusion.7
  375.0 1.6 multiply_reduce_fusion.4
  376.6 9.1 all-reduce.6
  387.1 1.3 subtract_convert_fusion
  388.4 1.0 fusion.50
  389.8 1.0 convolution_bitcast_fusion.1
  390.8 1.1 convolution_bitcast_fusion
  392.8 1.3 dynamic-slice
  398.2 341.4 %all-reduce.13.cloned.1.call-done = (f32[512,256]{0,1:T(8,128)}, f32[512,256]{0,1:T(8,128)}, f32[256,512]{1,0:T(8,128)}) async-done(((f32[512,256]{0,1:T(8,128)}, f32[512,256]{0,1:T(8,128)}, f32[256,512]{1,0:T(8,128)}), (f32[512,256]{0,1:T(8,128)}, f32[512,256]{0,1:T(8,128)}, f32[256,512]{1,0:T(8,128)})) %all-reduce.13.cloned.1.call-update) | async-done | bytes 1572880 | tf_op jit(solution)/shard_map/psum | solution.py:180
  739.7 1.3 multiply_reduce_fusion.1
  746.8 1.0 convolution_add_fusion.3
  748.3 1.0 fusion.1
  749.4 1.1 fusion
  750.8 1.0 copy.29
  758.7 341.2 %all-reduce.11.cloned.1.call-done = (f32[512,256]{0,1:T(8,128)}, f32[512,256]{0,1:T(8,128)}, f32[256,512]{1,0:T(8,128)}) async-done(((f32[512,256]{0,1:T(8,128)}, f32[512,256]{0,1:T(8,128)}, f32[256,512]{1,0:T(8,128)}), (f32[512,256]{0,1:T(8,128)}, f32[512,256]{0,1:T(8,128)}, f32[256,512]{1,0:T(8,128)})) %all-reduce.11.cloned.1.call-update) | async-done | bytes 1572880
  1100.0 1.1 fusion.28
  1101.8 1.4 fusion.43
  1103.2 1.4 fusion.41
  (158 shorter events, 29.3 us)
Async XLA Ops:
  7.2 360.7 %all-reduce.15.cloned.1.call-start = ((), (), s32[]{:S(2)}) async-start(), calls=%async_computation.2 | async-start | bytes 3145728 | tf_op jit(solution)/shard_map/psum | solution.py:157
  8.1 1.3 copy-start.1
  8.1 1.3 copy-start.5
  11.4 1.1 copy-start.25
  11.4 2.1 copy-start.23
  14.6 725.1 %all-reduce.13.cloned.1.call-start = ((), (), s32[]{:S(2)}) async-start(), calls=%async_computation.1 | async-start | bytes 3145728 | tf_op jit(solution)/shard_map/psum | solution.py:180
  367.9 1.9 copy-start.3
  372.2 1.7 copy-start.14
  374.9 1.7 copy-start.27
  387.1 1.3 copy-start.28
  388.4 1.1 copy-start.32
  388.4 1.1 copy-start.55
  389.8 1.1 copy-start.21
  389.8 1.1 copy-start.19
  391.9 708.1 %all-reduce.11.cloned.1.call-start = ((), (), s32[]{:S(2)}) async-start(), calls=%async_computation | async-start | bytes 3145728
  739.7 1.3 copy-start.44
  739.7 1.3 copy-start.46
  739.7 1.9 copy-start.11
  741.6 1.2 copy-start.12
  741.6 1.2 copy-start.38
  743.7 4.1 copy-start.9
  746.8 1.1 copy-start.54
  752.7 2.5 copy-start.8
  752.7 2.5 copy-start.13
  (35 other events, 28.9 us)
Sparse Core Ops, SparseCore 0:
  14.7 353.1 all-reduce.14
  392.0 347.5 all-reduce.12
  751.9 347.9 all-reduce.10
where the time goes:
time: 1110 us
  waiting for transfers between devices  1030 us (93%)
  matrix products  20.1 us (2%)
  local copies, waits for them, and re-layouts  18.2 us (2%)
  between operations  15.5 us (1%)
  other arithmetic  14.1 us (1%)
    psum x1, waiting for transfers between devices, per_device(): lax.psum((local_updates[0], local_updates[1], local_updates[2]), 'tok')  351 us
    psum x1, waiting for transfers between devices, per_device(): fast_grads = lax.psum((fast_parts[0], fast_parts[1], fast_parts[2]), 'tok')  341 us
    unnamed x4, waiting for transfers between devices  341 us
  transfers between devices with their start and end apart: 3, of which 3 were waited for; matrix products, arithmetic and copies ran while one was open for 1% of the time, Pallas kernels for 0%

commit v1 on v0

v1 whole, which is shorter than its diff:
```python
import jax
import jax.numpy as jnp
from jax import lax
from jax.experimental import pallas as pl
from jax.experimental.pallas import tpu as pltpu
from jax.sharding import PartitionSpec as P

EPSILON = 1e-06
CORES = 2
XS = 4
LANE = 128
BF = jnp.bfloat16
F32 = jnp.float32
MESH = pl.DeviceIdType.MESH
PIECES = ((0,), (1, 2))


def nn(a, b):
    return lax.dot_general(a, b, (((1,), (0,)), ((), ())), preferred_element_type=F32)


def nt(a, b):
    return lax.dot_general(a, b, (((1,), (1,)), ((), ())), preferred_element_type=F32)


def tn(a, b):
    return lax.dot_general(a, b, (((0,), (0,)), ((), ())), preferred_element_type=F32)


def log2(n):
    return n.bit_length() - 1


class Layout:
    def __init__(self, n, zs):
        self.n, self.zs = n, zs
        self.r = n // (CORES * XS * zs)
        self.rows = self.r * zs

    def natural(self, pos):
        lz, lr, lx, lc = log2(self.zs), log2(self.r), log2(XS), log2(CORES)
        z = pos & (self.zs - 1)
        r = lax.shift_right_logical(pos, lz) & (self.r - 1)
        x = lax.shift_right_logical(pos, lz + lr) & (XS - 1)
        c = lax.shift_right_logical(pos, lz + lr + lx) & (CORES - 1)
        return (z << (lx + lc + lr)) | (x << (lc + lr)) | (c << lr) | r

    def onehot(self):
        shape = (self.n, self.n)
        rows = lax.broadcasted_iota(jnp.int32, shape, 0)
        cols = self.natural(lax.broadcasted_iota(jnp.int32, shape, 1))
        return jnp.where(rows == cols, 1.0, 0.0).astype(BF)

    def onehot_t(self):
        shape = (self.n, self.n)
        rows = self.natural(lax.broadcasted_iota(jnp.int32, shape, 0))
        cols = lax.broadcasted_iota(jnp.int32, shape, 1)
        return jnp.where(rows == cols, 1.0, 0.0).astype(BF)


def body(heads, toks, q_ref, k_ref, v_ref, g_ref, rate_ref, gain_ref, w1_ref, w3_ref, w2_ref,
         qo_ref, ko_ref, vo_ref, own_ref, s):
    T, DH = q_ref.shape
    FH = w1_ref.shape[1]
    Z = toks // (CORES * XS)
    BR = DH * FH // (CORES * XS * LANE)
    NS = BR // Z
    fl, dl = Layout(FH, Z), Layout(DH, Z)
    layouts = (dl, fl, fl)
    JS = (FH // LANE, DH // LANE, DH // LANE)
    h = lax.axis_index("head")
    t = lax.axis_index("tok")
    c = lax.rem(t, CORES)
    x = lax.rem(t // CORES, XS)
    z = t // (CORES * XS)

    def at(c_, x_, z_):
        return (h, (z_ * XS + x_) * CORES + c_)

    other = at(1 - c, x, z)

    def x_peer(k):
        return lax.rem(x + k, XS)

    def z_peer(k):
        return lax.rem(z + k, Z)

    def head_peer(k):
        return lax.rem(h + k, heads)

    def z_step(i):
        half = (i + 1) // 2
        return Z // 2 + jnp.where(lax.rem(i, 2) == 0, half, -half)

    x_order = sorted(range(1, XS), key=lambda k: -min(k, XS - k))

    barrier = pltpu.get_barrier_semaphore()
    pl.semaphore_signal(barrier, inc=1, device_id=other, device_id_type=MESH)
    for k in range(1, XS):
        pl.semaphore_signal(barrier, inc=1, device_id=at(c, x_peer(k), z), device_id_type=MESH)

    def greet_z(k, carry):
        pl.semaphore_signal(barrier, inc=1, device_id=at(c, x, z_peer(k)), device_id_type=MESH)
        return carry

    lax.fori_loop(1, Z, greet_z, 0)
    for k in range(1, heads):
        pl.semaphore_signal(barrier, inc=1, device_id=(head_peer(k), t), device_id_type=MESH)

    RC = min(32, T)

    def each_rows(fn):
        def step(i, carry):
            fn(pl.ds(pl.multiple_of(i * RC, RC), RC))
            return carry

        lax.fori_loop(0, T // RC, step, 0)

    def remote(src, dst, send, recv, device):
        return pltpu.make_async_remote_copy(
            src_ref=src, dst_ref=dst, send_sem=send, recv_sem=recv, device_id=device, device_id_type=MESH
        )

    def wide(v, n):
        return jnp.concatenate([v] * (n // LANE), axis=1)

    def column(row):
        return jnp.broadcast_to(row, (LANE, row.shape[1])).T

    def parts(hidden):
        sg = jax.nn.sigmoid(hidden)
        return sg, hidden * sg, sg * (1.0 + hidden * (1.0 - sg))

    def put(ph, m, val):
        pc, mi = s.place[m]
        lay, js = layouts[m], JS[m]
        ref = s.sb[ph][pc]
        for cx in range(CORES * XS):
            for j in range(js):
                lo = mi * BR + j * lay.rows
                ref[cx // XS, cx % XS, lo:lo + lay.rows, :] = val[
                    cx * lay.rows:(cx + 1) * lay.rows, j * LANE:(j + 1) * LANE
                ].astype(BF)

    def rs_core(ph, pc):
        remote(s.sb[ph][pc].at[1 - c], s.cr[ph][pc], s.sems.at[ph, pc, 0], s.sems.at[ph, pc, 1], other).start()

    def rs_x(ph, pc):
        sb, cr, xs, xr = s.sb[ph][pc], s.cr[ph][pc], s.xs[ph][pc], s.xr[ph][pc]
        remote(sb.at[1 - c], cr, s.sems.at[ph, pc, 0], s.sems.at[ph, pc, 1], other).wait_recv()
        for k in x_order:
            xd = x_peer(k)
            xs[xd] = (sb[c, xd].astype(F32) + cr[xd].astype(F32)).astype(BF)
            remote(
                xs.at[xd], xr.at[x], s.sems.at[ph, pc, 2], s.sems.at[ph, pc, 3], at(c, xd, z)
            ).start()
        s.acc[pc][...] = sb[c, x].astype(F32) + cr[x].astype(F32)

    def rs_z(ph, pc):
        xr, zs, zr = s.xr[ph][pc], s.zs[ph][pc], s.zr[ph][pc]
        span = xr.at[pl.ds(0, XS - 1)]
        remote(span, span, s.sems.at[ph, pc, 2], s.sems.at[ph, pc, 3], other).wait_recv()
        total = s.acc[pc][...]
        for k in range(1, XS):
            total = total + xr[x_peer(k)].astype(F32)
        total = total.astype(BF)
        for mi in range(len(PIECES[pc])):
            chunks = nn(s.perm[...], total[mi * BR:(mi + 1) * BR])
            zs[:, mi * NS:(mi + 1) * NS, :] = chunks.reshape(Z, NS, LANE).astype(BF)

        def send(i, carry):
            zd = z_peer(z_step(i))
            remote(
                zs.at[zd], zr.at[z], s.sems.at[ph, pc, 4], s.sems.at[ph, pc, 5], at(c, x, zd)
            ).start()
            return carry

        lax.fori_loop(0, Z - 1, send, 0)

    def rs_own(ph, pc):
        zs, zr = s.zs[ph][pc], s.zr[ph][pc]
        span = zr.at[pl.ds(0, Z - 1)]
        remote(span, span, s.sems.at[ph, pc, 4], s.sems.at[ph, pc, 5], other).wait_recv()
        total = zs[z].astype(F32)
        for k in range(1, Z):
            total = total + zr[z_peer(k)].astype(F32)
        return [total[mi * NS:(mi + 1) * NS] for mi in range(len(PIECES[pc]))]

    def rs_drain(ph):
        for pc in range(len(PIECES)):
            sb, xr, zr = s.sb[ph][pc], s.xr[ph][pc], s.zr[ph][pc]
            for i, span in ((0, sb.at[1 - c]), (2, xr.at[pl.ds(0, XS - 1)]), (4, zr.at[pl.ds(0, Z - 1)])):
                remote(span, span, s.sems.at[ph, pc, i], s.sems.at[ph, pc, i + 1], other).wait_send()

    def ag_z(ph, pc, vals):
        ab, base = s.ab[ph][pc], 3 + ph
        for mi, val in enumerate(vals):
            ab[c, x, z, mi * NS:(mi + 1) * NS, :] = val.astype(BF)

        def send(i, carry):
            zd = z_peer(z_step(i))
            mine = ab.at[c, x, z]
            remote(mine, mine, s.sems.at[base, pc, 4], s.sems.at[base, pc, 5], at(c, x, zd)).start()
            return carry

        lax.fori_loop(0, Z - 1, send, 0)

    def ag_x(ph, pc):
        ab, base = s.ab[ph][pc], 3 + ph
        span = ab.at[c, x, pl.ds(0, Z - 1)]
        remote(span, span, s.sems.at[base, pc, 4], s.sems.at[base, pc, 5], other).wait_recv()
        mine = ab.at[c, x]
        for k in x_order:
            remote(
                mine, mine, s.sems.at[base, pc, 2], s.sems.at[base, pc, 3], at(c, x_peer(k), z)
            ).start()

    def ag_core(ph, pc):
        ab, base = s.ab[ph][pc], 3 + ph
        span = ab.at[c, pl.ds(0, XS - 1)]
        remote(span, span, s.sems.at[base, pc, 2], s.sems.at[base, pc, 3], other).wait_recv()
        mine = ab.at[c]
        remote(mine, mine, s.sems.at[base, pc, 0], s.sems.at[base, pc, 1], other).start()

    def unpack(ph, pc, cc, dst):
        ab = s.ab[ph][pc]

        def step(xx, carry):
            for mi, m in enumerate(PIECES[pc]):
                lay, js = layouts[m], JS[m]
                block = ab[cc, xx, :, mi * NS:(mi + 1) * NS, :].astype(F32).reshape(BR, LANE).astype(BF)
                rows = nn(s.permt[...], block).astype(BF)
                lo = pl.multiple_of((cc * XS + xx) * lay.rows, lay.rows)
                for j in range(js):
                    dst[m][pl.ds(lo, lay.rows), j * LANE:(j + 1) * LANE] = rows[j * lay.rows:(j + 1) * lay.rows]
            return carry

        lax.fori_loop(0, XS, step, 0)

    def ag_finish(ph, dst):
        for pc in range(len(PIECES)):
            unpack(ph, pc, c, dst)
        for pc in range(len(PIECES)):
            ab, base = s.ab[ph][pc], 3 + ph
            theirs = ab.at[1 - c]
            remote(theirs, theirs, s.sems.at[base, pc, 0], s.sems.at[base, pc, 1], other).wait_recv()
            unpack(ph, pc, 1 - c, dst)

    def ag_drain(ph):
        base = 3 + ph
        for pc in range(len(PIECES)):
            ab = s.ab[ph][pc]
            for i, span in ((0, ab.at[c]), (2, ab.at[c, pl.ds(0, XS - 1)]), (4, ab.at[c, x, pl.ds(0, Z - 1)])):
                remote(span, span, s.sems.at[base, pc, i], s.sems.at[base, pc, i + 1], other).wait_send()

    def colsum(val, r):
        total = jnp.broadcast_to(jnp.sum(val, axis=1, keepdims=True), (NS, LANE))
        shift = r
        while shift < NS:
            total = total + pltpu.roll(total, shift, 0)
            shift *= 2
        return total

    pieces = range(len(PIECES))

    rows_i = lax.broadcasted_iota(jnp.int32, (BR, BR), 0)
    cols_i = lax.broadcasted_iota(jnp.int32, (BR, BR), 1)
    lz, ln = log2(Z), log2(NS)
    s.perm[...] = jnp.where(
        cols_i == (((rows_i & (NS - 1)) << lz) | lax.shift_right_logical(rows_i, ln)), 1.0, 0.0
    ).astype(BF)
    s.permt[...] = jnp.where(
        rows_i == (((cols_i & (NS - 1)) << lz) | lax.shift_right_logical(cols_i, ln)), 1.0, 0.0
    ).astype(BF)
    s.pd[...] = dl.onehot()
    pft = fl.onehot_t()
    w1t, w3t, w2t = s.w1t, s.w3t, s.w2t
    w1t[...] = nt(pft, w1_ref[...]).astype(BF)
    w3t[...] = nt(pft, w3_ref[...]).astype(BF)
    w2t[...] = tn(nn(w2_ref[...], s.pd[...]).astype(BF), fl.onehot()).astype(BF)
    s.rate[...] = column(rate_ref[...])

    def scale_v(rows):
        s.vn[rows, :] = (-wide(s.rate[rows, :], DH) * v_ref[rows, :].astype(F32)).astype(BF)

    each_rows(scale_v)
    s.vp[...] = nn(s.vn[...], s.pd[...]).astype(BF)

    s.gp[...] = nt(k_ref[...], w1t[...])
    s.up[...] = nt(k_ref[...], w3t[...])

    def mix(rows):
        _, silu, _ = parts(s.gp[rows, :])
        s.mixed[rows, :] = (silu * s.up[rows, :]).astype(BF)

    each_rows(mix)
    put(0, 0, tn(s.vp[...], s.mixed[...]))
    waits = 1 + (XS - 1) + (Z - 1) + (heads - 1)
    pl.semaphore_wait(barrier, waits)
    rs_core(0, 0)
    s.db[...] = nn(s.vp[...], w2t[...])

    def backs(rows):
        _, silu, slope = parts(s.gp[rows, :])
        db = s.db[rows, :]
        s.gb[rows, :] = (db * s.up[rows, :] * slope).astype(BF)
        s.ub[rows, :] = (db * silu).astype(BF)

    each_rows(backs)
    put(0, 1, tn(s.gb[...], k_ref[...]))
    put(0, 2, tn(s.ub[...], k_ref[...]))
    rs_core(0, 1)
    for pc in pieces:
        rs_x(0, pc)
    for pc in pieces:
        rs_z(0, pc)

    priors = [None] * 3
    for m, wt in ((0, w2t), (1, w1t), (2, w3t)):
        lay, js = layouts[m], JS[m]
        lo = pl.multiple_of((c * XS + x) * lay.rows, lay.rows)
        block = jnp.concatenate(
            [wt[pl.ds(lo, lay.rows), j * LANE:(j + 1) * LANE] for j in range(js)], axis=0
        )
        s.prior[...] = nn(s.perm[...], block)
        priors[m] = s.prior[pl.ds(pl.multiple_of(z * NS, NS), NS), :]
    gain = gain_ref[...]
    high = gain.astype(BF).astype(F32)
    middle = (gain - high).astype(BF).astype(F32)
    low = gain - high - middle
    row8 = lax.broadcasted_iota(jnp.int32, (8, DH), 0)
    split = jnp.where(row8 == 0, high, jnp.where(row8 == 1, middle, jnp.where(row8 == 2, low, 0.0)))
    gain_p = jnp.sum(nn(split.astype(BF), s.pd[...]), axis=0, keepdims=True)
    s.gw[...] = nn(g_ref[...], s.pd[...]) * gain_p

    sums = [None] * 3
    moved, prior_norm, moved_norm = [None] * 3, [None] * 3, [None] * 3
    for m in range(3):
        prior_norm[m] = jnp.sqrt(colsum(priors[m] * priors[m], layouts[m].r) + EPSILON)
    for pc in pieces:
        got = rs_own(0, pc)
        fast = []
        for mi, m in enumerate(PIECES[pc]):
            moved[m] = priors[m] - got[mi]
            moved_norm[m] = jnp.sqrt(colsum(moved[m] * moved[m], layouts[m].r) + EPSILON)
            fast.append(moved[m] * (prior_norm[m] / moved_norm[m]))
        ag_z(0, pc, fast)
    for pc in pieces:
        ag_x(0, pc)
    for pc in pieces:
        ag_core(0, pc)
    f1t, f3t, f2t = s.f1t, s.f3t, s.f2t
    ag_finish(0, (f2t, f1t, f3t))

    s.qg[...] = nt(q_ref[...], f1t[...])
    s.qu[...] = nt(q_ref[...], f3t[...])

    def qmix(rows):
        _, silu, _ = parts(s.qg[rows, :])
        s.qm[rows, :] = (silu * s.qu[rows, :]).astype(BF)

    each_rows(qmix)
    s.out[...] = nt(s.qm[...], f2t[...])

    def fold(rows):
        o, w = s.out[rows, :], s.gw[rows, :]
        sq, dt = o * o, w * o
        s.sq[rows, :] = sum(sq[:, j * LANE:(j + 1) * LANE] for j in range(DH // LANE))
        s.dt[rows, :] = sum(dt[:, j * LANE:(j + 1) * LANE] for j in range(DH // LANE))

    each_rows(fold)
    row_sq = jnp.sum(s.sq[...].T, axis=0, keepdims=True)
    row_dt = jnp.sum(s.dt[...].T, axis=0, keepdims=True)
    row8t = lax.broadcasted_iota(jnp.int32, (8, T), 0)
    s.hs[...] = jnp.where(row8t == 0, row_sq, row_dt)
    for k in range(1, heads):
        remote(s.hs, s.hr.at[h], s.hsem.at[0], s.hsem.at[1], (head_peer(k), t)).start()
    span = s.hr.at[pl.ds(0, heads - 1)]
    remote(span, span, s.hsem.at[0], s.hsem.at[1], other).wait_recv()
    both = s.hs[...]
    for k in range(1, heads):
        both = both + s.hr[head_peer(k)]
    full_width = heads * DH
    square, dots = both[0:1], both[1:2]
    inverse = lax.rsqrt(square / full_width + EPSILON)
    s.inv[...] = column(inverse)
    s.coef[...] = column(inverse * inverse * inverse * dots / full_width)

    def outback(rows):
        s.ob[rows, :] = (
            wide(s.inv[rows, :], DH) * s.gw[rows, :] - s.out[rows, :] * wide(s.coef[rows, :], DH)
        ).astype(BF)

    each_rows(outback)

    put(1, 0, tn(s.ob[...], s.qm[...]))
    rs_core(1, 0)
    s.qb[...] = nn(s.ob[...], f2t[...])

    def qbacks(rows):
        _, silu, slope = parts(s.qg[rows, :])
        qb = s.qb[rows, :]
        s.qgb[rows, :] = (qb * s.qu[rows, :] * slope).astype(BF)
        s.qub[rows, :] = (qb * silu).astype(BF)

    each_rows(qbacks)
    put(1, 1, tn(s.qgb[...], q_ref[...]))
    put(1, 2, tn(s.qub[...], q_ref[...]))
    rs_core(1, 1)
    for pc in pieces:
        rs_x(1, pc)
    for pc in pieces:
        rs_z(1, pc)
    qo_ref[...] = (nn(s.qgb[...], f1t[...]) + nn(s.qub[...], f3t[...])).astype(BF)

    owned = [None] * 3
    for pc in pieces:
        got = rs_own(1, pc)
        cot = []
        for mi, m in enumerate(PIECES[pc]):
            grad, mn, pn = got[mi], moved_norm[m], prior_norm[m]
            dot = colsum(grad * moved[m], layouts[m].r)
            moved_grad = pn / mn * (grad - moved[m] * (dot / (mn * mn)))
            owned[m] = moved_grad + priors[m] * (dot / (mn * pn))
            cot.append(moved_grad)
        ag_z(1, pc, cot)
    for pc in pieces:
        ag_x(1, pc)
    for pc in pieces:
        ag_core(1, pc)
    c1t, c3t, c2t = s.c1t, s.c3t, s.c2t
    ag_finish(1, (c2t, c1t, c3t))

    s.qg[...] = nt(k_ref[...], c1t[...])
    s.qu[...] = nt(k_ref[...], c3t[...])
    s.qb[...] = nn(s.vp[...], c2t[...])

    def bars(rows):
        hidden, up, db = s.gp[rows, :], s.up[rows, :], s.db[rows, :]
        gate_bar, up_bar, mixed_bar = s.qg[rows, :], s.qu[rows, :], s.qb[rows, :]
        sg, silu, slope = parts(hidden)
        curve = sg * (1.0 - sg) * (2.0 + hidden * (1.0 - 2.0 * sg))
        s.dbb[rows, :] = (gate_bar * up * slope + up_bar * silu).astype(BF)
        s.qub[rows, :] = (gate_bar * db * slope + mixed_bar * silu).astype(BF)
        s.qgb[rows, :] = ((up_bar * db + mixed_bar * up) * slope + gate_bar * db * up * curve).astype(BF)

    each_rows(bars)
    put(2, 0, tn(s.vp[...], s.dbb[...]))
    rs_core(2, 0)
    put(2, 1, tn(s.qgb[...], k_ref[...]))
    put(2, 2, tn(s.qub[...], k_ref[...]))
    rs_core(2, 1)
    for pc in pieces:
        rs_x(2, pc)
    for pc in pieces:
        rs_z(2, pc)

    s.out[...] = nt(s.mixed[...], c2t[...]) + nt(s.dbb[...], w2t[...])

    def value(rows):
        s.vn[rows, :] = (wide(s.rate[rows, :], DH) * s.out[rows, :]).astype(BF)

    each_rows(value)
    vo_ref[...] = nt(s.vn[...], s.pd[...]).astype(BF)
    ko_ref[...] = (
        -(nn(s.gb[...], c1t[...]) + nn(s.ub[...], c3t[...]) + nn(s.qgb[...], w1t[...]) + nn(s.qub[...], w3t[...]))
    ).astype(BF)

    for pc in pieces:
        got = rs_own(2, pc)
        for mi, m in enumerate(PIECES[pc]):
            own_ref[m] = owned[m] - got[mi]
    for ph in range(3):
        rs_drain(ph)
    for ph in range(2):
        ag_drain(ph)
    hall = s.hr.at[pl.ds(0, heads - 1)]
    remote(hall, hall, s.hsem.at[0], s.hsem.at[1], other).wait_send()


class Scratch:
    def __init__(self, heads, toks, T, DH, FH):
        self.specs, self.names = [], []
        Z = toks // (CORES * XS)
        BR = DH * FH // (CORES * XS * LANE)
        NS = BR // Z

        def vm(name, *shape, dtype=BF):
            self.specs.append(pltpu.VMEM(shape, dtype))
            self.names.append(name)

        for name in ("gp", "up", "db", "qg", "qu", "qb"):
            vm(name, T, FH, dtype=F32)
        for name in ("mixed", "gb", "ub", "qm", "qgb", "qub", "dbb"):
            vm(name, T, FH)
        for name in ("vn", "vp", "ob"):
            vm(name, T, DH)
        for name in ("gw", "out"):
            vm(name, T, DH, dtype=F32)
        for name in ("rate", "inv", "coef", "sq", "dt"):
            vm(name, T, LANE, dtype=F32)
        for name in ("w1t", "w3t", "f1t", "f3t", "c1t", "c3t"):
            vm(name, FH, DH)
        for name in ("w2t", "f2t", "c2t"):
            vm(name, DH, FH)
        vm("pd", DH, DH)
        vm("perm", BR, BR)
        vm("permt", BR, BR)
        vm("prior", BR, LANE, dtype=F32)
        vm("hs", 8, T, dtype=F32)
        vm("hr", heads, 8, T, dtype=F32)
        for pc, ms in enumerate(PIECES):
            n = len(ms)
            vm(("acc", pc), n * BR, LANE, dtype=F32)
            for ph in range(3):
                vm(("sb", ph, pc), CORES, XS, n * BR, LANE)
                vm(("cr", ph, pc), XS, n * BR, LANE)
                vm(("xs", ph, pc), XS, n * BR, LANE)
                vm(("xr", ph, pc), XS, n * BR, LANE)
                vm(("zs", ph, pc), Z, n * NS, LANE)
                vm(("zr", ph, pc), Z, n * NS, LANE)
            for ph in range(2):
                vm(("ab", ph, pc), CORES, XS, Z, n * NS, LANE)
        for name, shape in (("sems", (5, len(PIECES), 6)), ("hsem", (2,))):
            self.specs.append(pltpu.SemaphoreType.DMA(shape))
            self.names.append(name)

    def bind(self, refs):
        class Refs:
            pass

        s = Refs()
        s.place = {m: (pc, mi) for pc, ms in enumerate(PIECES) for mi, m in enumerate(ms)}
        for name in ("sb", "cr", "xs", "xr", "zs", "zr"):
            setattr(s, name, [[None] * len(PIECES) for _ in range(3)])
        s.ab = [[None] * len(PIECES) for _ in range(2)]
        s.acc = [None] * len(PIECES)
        for name, ref in zip(self.names, refs):
            if isinstance(name, str):
                setattr(s, name, ref)
            elif len(name) == 2:
                s.acc[name[1]] = ref
            else:
                getattr(s, name[0])[name[1]][name[2]] = ref
        return s


def per_device(heads, toks, query, key, value, out_grad, rates, gain, w1, w3, w2):
    T, DH = query.shape
    FH = w1.shape[2]
    Z = toks // (CORES * XS)
    NS = DH * FH // (CORES * XS * LANE) // Z
    scratch = Scratch(heads, toks, T, DH, FH)

    def kernel(*refs):
        body(heads, toks, *refs[:13], scratch.bind(refs[13:]))

    vmem = pl.BlockSpec(memory_space=pltpu.VMEM)
    tokens = jax.ShapeDtypeStruct((T, DH), BF)
    qo, ko, vo, own = pl.pallas_call(
        kernel,
        out_shape=(tokens, tokens, tokens, jax.ShapeDtypeStruct((3, NS, LANE), F32)),
        in_specs=[vmem] * 9,
        out_specs=(vmem,) * 4,
        scratch_shapes=scratch.specs,
        compiler_params=pltpu.CompilerParams(
            collective_id=0, has_side_effects=True, vmem_limit_bytes=56 * 1024 * 1024
        ),
        name="lact_backward",
    )(query, key, value, out_grad, rates.reshape(1, T), gain.reshape(1, DH), w1[0], w3[0], w2[0])
    fr, dr = Layout(FH, Z).r, Layout(DH, Z).r
    down = own[0].reshape(FH // LANE, dr, LANE).transpose(0, 2, 1).reshape(CORES, XS, fr, Z, dr)
    down = down.transpose(3, 1, 0, 2, 4).reshape(1, FH, dr)
    gate = own[1].reshape(DH // LANE, fr, LANE).transpose(0, 2, 1).reshape(1, DH, fr)
    up = own[2].reshape(DH // LANE, fr, LANE).transpose(0, 2, 1).reshape(1, DH, fr)
    return qo, ko, vo, gate, up, down


def solution(mesh):
    heads, toks = mesh.shape["head"], mesh.shape["tok"]
    token_spec, weight_in, weight_out = P("tok", "head"), P("head", None, None), P("head", None, "tok")

    def step(*args):
        return per_device(heads, toks, *args)

    return jax.shard_map(
        step,
        mesh=mesh,
        in_specs=(token_spec,) * 5 + (P("head"),) + (weight_in,) * 3,
        out_specs=(token_spec,) * 3 + (weight_out,) * 3,
        check_vma=False,
    )
```

time: 1110 us -> 105 us (0.09)
  waiting for transfers between devices: 1030 us -> 0 us
  Pallas kernels: 0 us -> 99.1 us
  matrix products: 20.1 us -> 0 us
  between operations: 15.5 us -> 0.67 us
  other arithmetic: 14.1 us -> 0 us
  local copies, waits for them, and re-layouts: 18.2 us -> 5.1 us
    psum x2 -> x0, waiting for transfers between devices: 693 us -> none  [the longest x1 351 us: per_device(): lax.psum((local_updates[0], local_updates[1], local_updates[2]), 'tok')]
    unnamed x4 -> x0, waiting for transfers between devices: 341 us -> none
    pallas_call x0 -> x1, Pallas kernels: none -> 99.1 us  [per_device(): pl.pallas_call(kernel, out_shape=(tokens, tokens, tokens, jax.ShapeDtypeS...]
    dot_general x27 -> x0, matrix products: 20.1 us -> none  [the longest x9 8.81 us: contract_rows(): lax.dot_general(first_op, second_op, (((0,), (0,)), ((), ())), preferred_...]
    unnamed x116 -> x10, local copies, waits for them, and re-layouts: 16.3 us -> 3.47 us
  transfers between devices with their start and end apart: 3 -> 0, of which waited for: 3 -> 0; matrix products, arithmetic and copies ran while one was open for 1% -> 0% of each run, Pallas kernels for 0% -> 0%
where the time goes in v1:
time: 105 us
  Pallas kernels  99.1 us (94%)
  local copies, waits for them, and re-layouts  5.1 us (5%)
    pallas_call x1, Pallas kernels, per_device(): pl.pallas_call(kernel, out_shape=(tokens, tokens, tokens, jax.ShapeDtypeS...  99.1 us
    unnamed x10, local copies, waits for them, and re-layouts  3.47 us

profile of v1, /device:TPU:1, one launch (start us, length us, event | category | flops | bytes accessed | tf_op | source)
XLA Modules:
  0.0 104.8 jit_solution(3172322333171881572)
XLA Ops:
  0.6 99.1 %lact_backward.1 = (bf16[256,512]{1,0:T(8,128)(2,1)}, bf16[256,512]{1,0:T(8,128)(2,1)}, bf16[256,512]{1,0:T(8,128)(2,1)}, f32[3,8,128]{2,1,0:T(8,128)}) custom-call(bf16[256,512]{1,0:T(8,128)(2,1)} %refs_0_.1, bf16[256,512]{1,0:T(8,128)(2,1)} %refs_1_.1, bf16[256,512]{1,0:T(8,128)(2,1)} %refs_2_.1, bf16[256,512]{1,0:T(8,128)(2,1)} %refs_3_.1, ...), custom_call_target="tpu_custom_call" | custom-call | tf_op jit(solution)/shard_map/lact_backward/pallas_call | solution.py:560
  99.7 0.0 copy-start.2
  99.7 1.3 %fusion = (f32[1,8,128]{2,1,0:T(8,128)S(1)}, f32[1,8,128]{2,1,0:T(8,128)}, f32[1,8,128]{2,1,0:T(8,128)}) fusion(f32[3,8,128]{2,1,0:T(8,128)} %get-tuple-element.13), kind=kLoop, calls=%fused_computation | loop fusion | bytes 24576 | tf_op jit(solution)/shard_map/slice | solution.py:572
  101.0 0.1 reshape.34
  101.1 0.2 copy.23
  101.4 0.7 copy.24
  102.0 0.0 copy-done.2
  102.0 0.0 copy-start.1
  102.0 0.7 copy.28
  102.7 0.3 copy-done.1
  103.1 0.0 copy-start
  103.1 0.7 copy.29
  103.8 0.3 copy-done
  104.1 0.7 copy.30
Async XLA Ops:
  99.7 2.3 %copy-start.2 = (bf16[256,512]{1,0:T(8,128)(2,1)S(1)}, bf16[256,512]{1,0:T(8,128)(2,1)}, u32[]{:S(2)}) copy-start(bf16[256,512]{1,0:T(8,128)(2,1)} %get-tuple-element.35) | copy-start | bytes 786436
  102.0 1.0 copy-start.1
  103.1 1.0 copy-start

commit v2 on v1

--- a/solution.py
+++ b/solution.py
@@ -12,7 +12,8 @@
 BF = jnp.bfloat16
 F32 = jnp.float32
 MESH = pl.DeviceIdType.MESH
-PIECES = ((0,), (1, 2))
+VMEM_LIMIT = 56 * 1024 * 1024
+PIECES = ((0,), (1,), (2,))
 
 
 def nn(a, b):
@@ -58,8 +59,11 @@
         return jnp.where(rows == cols, 1.0, 0.0).astype(BF)
 
 
-def body(heads, toks, q_ref, k_ref, v_ref, g_ref, rate_ref, gain_ref, w1_ref, w3_ref, w2_ref,
-         qo_ref, ko_ref, vo_ref, own_ref, s):
+INPUTS = ("w1", "w3", "k", "w2", "rate_row", "v", "g", "gain_row", "q")
+
+
+def body(heads, toks, ins, outs, s):
+    q_ref, k_ref, v_ref, g_ref, w1_ref, w3_ref, w2_ref = s.q, s.k, s.v, s.g, s.w1, s.w3, s.w2
     T, DH = q_ref.shape
     FH = w1_ref.shape[1]
     Z = toks // (CORES * XS)
@@ -94,18 +98,29 @@
 
     x_order = sorted(range(1, XS), key=lambda k: -min(k, XS - k))
 
+    loads = {}
+    for i, name in enumerate(INPUTS):
+        loads[name] = pltpu.make_async_copy(ins[name], getattr(s, name), s.insem.at[i])
+
     barrier = pltpu.get_barrier_semaphore()
-    pl.semaphore_signal(barrier, inc=1, device_id=other, device_id_type=MESH)
-    for k in range(1, XS):
-        pl.semaphore_signal(barrier, inc=1, device_id=at(c, x_peer(k), z), device_id_type=MESH)
-
-    def greet_z(k, carry):
-        pl.semaphore_signal(barrier, inc=1, device_id=at(c, x, z_peer(k)), device_id_type=MESH)
-        return carry
-
-    lax.fori_loop(1, Z, greet_z, 0)
-    for k in range(1, heads):
-        pl.semaphore_signal(barrier, inc=1, device_id=(head_peer(k), t), device_id_type=MESH)
+    near = [other] + [at(c, x_peer(k), z) for k in range(1, XS)]
+    near += [at(c, x, z_peer(1)), at(c, x, z_peer(Z - 1))]
+    near += [(head_peer(k), t) for k in range(1, heads)]
+    for device in near:
+        pl.semaphore_signal(barrier, inc=1, device_id=device, device_id_type=MESH)
+    for name in INPUTS:
+        loads[name].start()
+
+    rounds = log2(Z) - 1
+
+    def reach_signal(i):
+        if i < rounds:
+            for k in (2**i, Z - 2**i):
+                pl.semaphore_signal(s.reach.at[i], inc=1, device_id=at(c, x, z_peer(k)), device_id_type=MESH)
+
+    def reach_wait(i):
+        if i < rounds:
+            pl.semaphore_wait(s.reach.at[i], 2)
 
     RC = min(32, T)
 
@@ -224,18 +239,18 @@
 
     def unpack(ph, pc, cc, dst):
         ab = s.ab[ph][pc]
-
-        def step(xx, carry):
-            for mi, m in enumerate(PIECES[pc]):
-                lay, js = layouts[m], JS[m]
-                block = ab[cc, xx, :, mi * NS:(mi + 1) * NS, :].astype(F32).reshape(BR, LANE).astype(BF)
-                rows = nn(s.permt[...], block).astype(BF)
+        for mi, m in enumerate(PIECES[pc]):
+            lay, js = layouts[m], JS[m]
+            blocks = jnp.concatenate(
+                [ab[cc, xx, :, mi * NS:(mi + 1) * NS, :].astype(F32).reshape(BR, LANE) for xx in range(XS)], axis=1
+            )
+            rows = nn(s.permt[...], blocks.astype(BF)).astype(BF)
+            for xx in range(XS):
                 lo = pl.multiple_of((cc * XS + xx) * lay.rows, lay.rows)
                 for j in range(js):
-                    dst[m][pl.ds(lo, lay.rows), j * LANE:(j + 1) * LANE] = rows[j * lay.rows:(j + 1) * lay.rows]
-            return carry
-
-        lax.fori_loop(0, XS, step, 0)
+                    dst[m][pl.ds(lo, lay.rows), j * LANE:(j + 1) * LANE] = rows[
+                        j * lay.rows:(j + 1) * lay.rows, xx * LANE:(xx + 1) * LANE
+                    ]
 
     def ag_finish(ph, dst):
         for pc in range(len(PIECES)):
@@ -272,20 +287,15 @@
     s.permt[...] = jnp.where(
         rows_i == (((cols_i & (NS - 1)) << lz) | lax.shift_right_logical(cols_i, ln)), 1.0, 0.0
     ).astype(BF)
-    s.pd[...] = dl.onehot()
     pft = fl.onehot_t()
     w1t, w3t, w2t = s.w1t, s.w3t, s.w2t
+    s.pd[...] = dl.onehot()
+    loads["w1"].wait()
     w1t[...] = nt(pft, w1_ref[...]).astype(BF)
+    loads["w3"].wait()
     w3t[...] = nt(pft, w3_ref[...]).astype(BF)
-    w2t[...] = tn(nn(w2_ref[...], s.pd[...]).astype(BF), fl.onehot()).astype(BF)
-    s.rate[...] = column(rate_ref[...])
-
-    def scale_v(rows):
-        s.vn[rows, :] = (-wide(s.rate[rows, :], DH) * v_ref[rows, :].astype(F32)).astype(BF)
-
-    each_rows(scale_v)
-    s.vp[...] = nn(s.vn[...], s.pd[...]).astype(BF)
-
+
+    loads["k"].wait()
     s.gp[...] = nt(k_ref[...], w1t[...])
     s.up[...] = nt(k_ref[...], w3t[...])
 
@@ -294,10 +304,21 @@
         s.mixed[rows, :] = (silu * s.up[rows, :]).astype(BF)
 
     each_rows(mix)
+    loads["rate_row"].wait()
+    s.rate[...] = column(s.rate_row[...])
+    loads["v"].wait()
+
+    def scale_v(rows):
+        s.vn[rows, :] = (-wide(s.rate[rows, :], DH) * v_ref[rows, :].astype(F32)).astype(BF)
+
+    each_rows(scale_v)
+    s.vp[...] = nn(s.vn[...], s.pd[...]).astype(BF)
     put(0, 0, tn(s.vp[...], s.mixed[...]))
-    waits = 1 + (XS - 1) + (Z - 1) + (heads - 1)
-    pl.semaphore_wait(barrier, waits)
+    pl.semaphore_wait(barrier, len(near))
+    reach_signal(0)
     rs_core(0, 0)
+    loads["w2"].wait()
+    w2t[...] = tn(nn(w2_ref[...], s.pd[...]).astype(BF), fl.onehot()).astype(BF)
     s.db[...] = nn(s.vp[...], w2t[...])
 
     def backs(rows):
@@ -308,10 +329,19 @@
 
     each_rows(backs)
     put(0, 1, tn(s.gb[...], k_ref[...]))
+    rs_core(0, 1)
     put(0, 2, tn(s.ub[...], k_ref[...]))
-    rs_core(0, 1)
-    for pc in pieces:
-        rs_x(0, pc)
+    rs_core(0, 2)
+    reach_wait(0)
+    reach_signal(1)
+    rs_x(0, 0)
+    rs_x(0, 1)
+    reach_wait(1)
+    reach_signal(2)
+    rs_x(0, 2)
+    for i in range(2, rounds):
+        reach_wait(i)
+        reach_signal(i + 1)
     for pc in pieces:
         rs_z(0, pc)
 
@@ -324,7 +354,10 @@
         )
         s.prior[...] = nn(s.perm[...], block)
         priors[m] = s.prior[pl.ds(pl.multiple_of(z * NS, NS), NS), :]
-    gain = gain_ref[...]
+    loads["gain_row"].wait()
+    loads["g"].wait()
+    loads["q"].wait()
+    gain = s.gain_row[...]
     high = gain.astype(BF).astype(F32)
     middle = (gain - high).astype(BF).astype(F32)
     low = gain - high - middle
@@ -405,13 +438,16 @@
 
     each_rows(qbacks)
     put(1, 1, tn(s.qgb[...], q_ref[...]))
+    rs_core(1, 1)
     put(1, 2, tn(s.qub[...], q_ref[...]))
-    rs_core(1, 1)
+    rs_core(1, 2)
     for pc in pieces:
         rs_x(1, pc)
     for pc in pieces:
         rs_z(1, pc)
-    qo_ref[...] = (nn(s.qgb[...], f1t[...]) + nn(s.qub[...], f3t[...])).astype(BF)
+    s.qo[...] = (nn(s.qgb[...], f1t[...]) + nn(s.qub[...], f3t[...])).astype(BF)
+    stores = [pltpu.make_async_copy(s.qo, outs[0], s.outsem.at[0])]
+    stores[0].start()
 
     owned = [None] * 3
     for pc in pieces:
@@ -448,8 +484,9 @@
     put(2, 0, tn(s.vp[...], s.dbb[...]))
     rs_core(2, 0)
     put(2, 1, tn(s.qgb[...], k_ref[...]))
+    rs_core(2, 1)
     put(2, 2, tn(s.qub[...], k_ref[...]))
-    rs_core(2, 1)
+    rs_core(2, 2)
     for pc in pieces:
         rs_x(2, pc)
     for pc in pieces:
@@ -461,21 +498,29 @@
         s.vn[rows, :] = (wide(s.rate[rows, :], DH) * s.out[rows, :]).astype(BF)
 
     each_rows(value)
-    vo_ref[...] = nt(s.vn[...], s.pd[...]).astype(BF)
-    ko_ref[...] = (
+    s.vo[...] = nt(s.vn[...], s.pd[...]).astype(BF)
+    stores.append(pltpu.make_async_copy(s.vo, outs[2], s.outsem.at[1]))
+    stores[1].start()
+    s.ko[...] = (
         -(nn(s.gb[...], c1t[...]) + nn(s.ub[...], c3t[...]) + nn(s.qgb[...], w1t[...]) + nn(s.qub[...], w3t[...]))
     ).astype(BF)
+    stores.append(pltpu.make_async_copy(s.ko, outs[1], s.outsem.at[2]))
+    stores[2].start()
 
     for pc in pieces:
         got = rs_own(2, pc)
         for mi, m in enumerate(PIECES[pc]):
-            own_ref[m] = owned[m] - got[mi]
+            s.own[m] = owned[m] - got[mi]
+    stores.append(pltpu.make_async_copy(s.own, outs[3], s.outsem.at[3]))
+    stores[3].start()
     for ph in range(3):
         rs_drain(ph)
     for ph in range(2):
         ag_drain(ph)
     hall = s.hr.at[pl.ds(0, heads - 1)]
     remote(hall, hall, s.hsem.at[0], s.hsem.at[1], other).wait_send()
+    for store in stores:
+        store.wait()
 
 
 class Scratch:
@@ -503,6 +548,14 @@
             vm(name, FH, DH)
         for name in ("w2t", "f2t", "c2t"):
             vm(name, DH, FH)
+        for name in ("q", "k", "v", "g", "qo", "ko", "vo"):
+            vm(name, T, DH)
+        vm("w1", DH, FH)
+        vm("w3", DH, FH)
+        vm("w2", FH, DH)
+        vm("rate_row", 1, T, dtype=F32)
+        vm("gain_row", 1, DH, dtype=F32)
+        vm("own", 3, NS, LANE, dtype=F32)
         vm("pd", DH, DH)
         vm("perm", BR, BR)
         vm("permt", BR, BR)
@@ -521,9 +574,13 @@
                 vm(("zr", ph, pc), Z, n * NS, LANE)
             for ph in range(2):
                 vm(("ab", ph, pc), CORES, XS, Z, n * NS, LANE)
-        for name, shape in (("sems", (5, len(PIECES), 6)), ("hsem", (2,))):
+        for name, shape in (
+            ("sems", (5, len(PIECES), 6)), ("hsem", (2,)), ("insem", (len(INPUTS),)), ("outsem", (4,))
+        ):
             self.specs.append(pltpu.SemaphoreType.DMA(shape))
             self.names.append(name)
+        self.specs.append(pltpu.SemaphoreType.REGULAR((max(1, log2(Z) - 1),)))
+        self.names.append("reach")
 
     def bind(self, refs):
         class Refs:
@@ -552,22 +609,28 @@
     NS = DH * FH // (CORES * XS * LANE) // Z
     scratch = Scratch(heads, toks, T, DH, FH)
 
+    arrays = dict(
+        q=query, k=key, v=value, g=out_grad, rate_row=rates.reshape(1, T), gain_row=gain.reshape(1, DH),
+        w1=w1[0], w3=w3[0], w2=w2[0],
+    )
+
     def kernel(*refs):
-        body(heads, toks, *refs[:13], scratch.bind(refs[13:]))
-
-    vmem = pl.BlockSpec(memory_space=pltpu.VMEM)
+        n = len(INPUTS)
+        body(heads, toks, dict(zip(INPUTS, refs[:n])), refs[n:n + 4], scratch.bind(refs[n + 4:]))
+
+    anywhere = pl.BlockSpec(memory_space=pl.ANY)
     tokens = jax.ShapeDtypeStruct((T, DH), BF)
     qo, ko, vo, own = pl.pallas_call(
         kernel,
         out_shape=(tokens, tokens, tokens, jax.ShapeDtypeStruct((3, NS, LANE), F32)),
-        in_specs=[vmem] * 9,
-        out_specs=(vmem,) * 4,
+        in_specs=[anywhere] * len(INPUTS),
+        out_specs=(anywhere,) * 4,
         scratch_shapes=scratch.specs,
         compiler_params=pltpu.CompilerParams(
-            collective_id=0, has_side_effects=True, vmem_limit_bytes=56 * 1024 * 1024
+            collective_id=0, has_side_effects=True, vmem_limit_bytes=VMEM_LIMIT
         ),
         name="lact_backward",
-    )(query, key, value, out_grad, rates.reshape(1, T), gain.reshape(1, DH), w1[0], w3[0], w2[0])
+    )(*(arrays[name] for name in INPUTS))
     fr, dr = Layout(FH, Z).r, Layout(DH, Z).r
     down = own[0].reshape(FH // LANE, dr, LANE).transpose(0, 2, 1).reshape(CORES, XS, fr, Z, dr)
     down = down.transpose(3, 1, 0, 2, 4).reshape(1, FH, dr)

time: 105 us -> 97.2 us (0.926)
  Pallas kernels: 99.1 us -> 91.2 us
    pallas_call x1, Pallas kernels: 99.1 us -> 91.2 us  [per_device(): pl.pallas_call(kernel, out_shape=(tokens, tokens, tokens, jax.ShapeDtypeS...]
where the time goes in v2:
time: 97.2 us; the launch traced here: 97 us
  Pallas kernels  91.2 us (94%)
  local copies, waits for them, and re-layouts  5.1 us (5%)
    pallas_call x1, Pallas kernels, per_device(): pl.pallas_call(kernel, out_shape=(tokens, tokens, tokens, jax.ShapeDtypeS...  91.2 us
    unnamed x10, local copies, waits for them, and re-layouts  3.47 us

profile of v2, /device:TPU:1, one launch (start us, length us, event | category | flops | bytes accessed | tf_op | source)
XLA Modules:
  0.0 97.0 jit_solution(2390155011889179836)
XLA Ops:
  0.6 91.2 %lact_backward.1 = (bf16[256,512]{1,0:T(8,128)(2,1)}, bf16[256,512]{1,0:T(8,128)(2,1)}, bf16[256,512]{1,0:T(8,128)(2,1)}, f32[3,8,128]{2,1,0:T(8,128)}) custom-call(bf16[512,256]{1,0:T(8,128)(2,1)} %bitcast.23, bf16[512,256]{1,0:T(8,128)(2,1)} %bitcast.24, bf16[256,512]{1,0:T(8,128)(2,1)} %refs_2_.1, bf16[256,512]{1,0:T(8,128)(2,1)} %bitcast.25, ...), custom_call_target="tpu_custom_call" | custom-call | tf_op jit(solution)/shard_map/lact_backward/pallas_call | solution.py:623
  91.8 0.0 copy-start.2
  91.9 1.3 %fusion = (f32[1,8,128]{2,1,0:T(8,128)S(1)}, f32[1,8,128]{2,1,0:T(8,128)}, f32[1,8,128]{2,1,0:T(8,128)}) fusion(f32[3,8,128]{2,1,0:T(8,128)} %get-tuple-element.13), kind=kLoop, calls=%fused_computation | loop fusion | bytes 24576 | tf_op jit(solution)/shard_map/slice | solution.py:635
  93.2 0.1 reshape.34
  93.3 0.2 copy.23
  93.5 0.7 copy.24
  94.2 0.0 copy-done.2
  94.2 0.0 copy-start.1
  94.2 0.7 copy.28
  94.9 0.3 copy-done.1
  95.2 0.0 copy-start
  95.2 0.7 copy.29
  95.9 0.3 copy-done
  96.3 0.7 copy.30
Async XLA Ops:
  91.8 2.3 %copy-start.2 = (bf16[256,512]{1,0:T(8,128)(2,1)S(1)}, bf16[256,512]{1,0:T(8,128)(2,1)}, u32[]{:S(2)}) copy-start(bf16[256,512]{1,0:T(8,128)(2,1)} %get-tuple-element.35) | copy-start | bytes 786436
  94.2 1.0 %copy-start.1 = (bf16[256,512]{1,0:T(8,128)(2,1)S(1)}, bf16[256,512]{1,0:T(8,128)(2,1)}, u32[]{:S(2)}) copy-start(bf16[256,512]{1,0:T(8,128)(2,1)} %get-tuple-element.36) | copy-start | bytes 786436
  95.2 1.0 %copy-start = (bf16[256,512]{1,0:T(8,128)(2,1)S(1)}, bf16[256,512]{1,0:T(8,128)(2,1)}, u32[]{:S(2)}) copy-start(bf16[256,512]{1,0:T(8,128)(2,1)} %get-tuple-element.37) | copy-start | bytes 786436

commit v3 on v2

--- a/solution.py
+++ b/solution.py
@@ -12,7 +12,7 @@
 BF = jnp.bfloat16
 F32 = jnp.float32
 MESH = pl.DeviceIdType.MESH
-VMEM_LIMIT = 56 * 1024 * 1024
+VMEM_LIMIT = 24 * 1024 * 1024
 PIECES = ((0,), (1,), (2,))
 
 
@@ -278,6 +278,19 @@
 
     pieces = range(len(PIECES))
 
+    def put_down(val):
+        high = val.astype(BF).astype(F32)
+        middle = (val - high).astype(BF).astype(F32)
+        low = val - high - middle
+        split = jnp.concatenate([high, middle, low, jnp.zeros_like(low)], axis=0).astype(BF)
+        total = None
+        for j in range(JS[0]):
+            part = nn(split, s.pft[j * LANE:(j + 1) * LANE, :])
+            part = part[0:NS] + part[NS:2 * NS] + part[2 * NS:3 * NS]
+            part = part[j * dl.r:(j + 1) * dl.r]
+            total = part if total is None else total + part
+        s.own0[...] = total
+
     rows_i = lax.broadcasted_iota(jnp.int32, (BR, BR), 0)
     cols_i = lax.broadcasted_iota(jnp.int32, (BR, BR), 1)
     lz, ln = log2(Z), log2(NS)
@@ -287,13 +300,13 @@
     s.permt[...] = jnp.where(
         rows_i == (((cols_i & (NS - 1)) << lz) | lax.shift_right_logical(cols_i, ln)), 1.0, 0.0
     ).astype(BF)
-    pft = fl.onehot_t()
+    s.pft[...] = fl.onehot_t()
     w1t, w3t, w2t = s.w1t, s.w3t, s.w2t
     s.pd[...] = dl.onehot()
     loads["w1"].wait()
-    w1t[...] = nt(pft, w1_ref[...]).astype(BF)
+    w1t[...] = nt(s.pft[...], w1_ref[...]).astype(BF)
     loads["w3"].wait()
-    w3t[...] = nt(pft, w3_ref[...]).astype(BF)
+    w3t[...] = nt(s.pft[...], w3_ref[...]).astype(BF)
 
     loads["k"].wait()
     s.gp[...] = nt(k_ref[...], w1t[...])
@@ -510,9 +523,15 @@
     for pc in pieces:
         got = rs_own(2, pc)
         for mi, m in enumerate(PIECES[pc]):
-            s.own[m] = owned[m] - got[mi]
-    stores.append(pltpu.make_async_copy(s.own, outs[3], s.outsem.at[3]))
-    stores[3].start()
+            final = owned[m] - got[mi]
+            if m == 0:
+                put_down(final)
+                stores.append(pltpu.make_async_copy(s.own0, outs[3], s.outsem.at[3]))
+            else:
+                own = (s.own1, s.own2)[m - 1]
+                own[...] = final
+                stores.append(pltpu.make_async_copy(own, outs[3 + m], s.outsem.at[3 + m]))
+            stores[-1].start()
     for ph in range(3):
         rs_drain(ph)
     for ph in range(2):
@@ -555,7 +574,10 @@
         vm("w2", FH, DH)
         vm("rate_row", 1, T, dtype=F32)
         vm("gain_row", 1, DH, dtype=F32)
-        vm("own", 3, NS, LANE, dtype=F32)
+        vm("own0", Layout(DH, Z).r, FH, dtype=F32)
+        vm("own1", NS, LANE, dtype=F32)
+        vm("own2", NS, LANE, dtype=F32)
+        vm("pft", FH, FH)
         vm("pd", DH, DH)
         vm("perm", BR, BR)
         vm("permt", BR, BR)
@@ -575,7 +597,7 @@
             for ph in range(2):
                 vm(("ab", ph, pc), CORES, XS, Z, n * NS, LANE)
         for name, shape in (
-            ("sems", (5, len(PIECES), 6)), ("hsem", (2,)), ("insem", (len(INPUTS),)), ("outsem", (4,))
+            ("sems", (5, len(PIECES), 6)), ("hsem", (2,)), ("insem", (len(INPUTS),)), ("outsem", (6,))
         ):
             self.specs.append(pltpu.SemaphoreType.DMA(shape))
             self.names.append(name)
@@ -616,26 +638,45 @@
 
     def kernel(*refs):
         n = len(INPUTS)
-        body(heads, toks, dict(zip(INPUTS, refs[:n])), refs[n:n + 4], scratch.bind(refs[n + 4:]))
-
-    anywhere = pl.BlockSpec(memory_space=pl.ANY)
+        body(heads, toks, dict(zip(INPUTS, refs[:n])), refs[n:n + 6], scratch.bind(refs[n + 6:]))
+
+    anywhere, hbm = pl.BlockSpec(memory_space=pl.ANY), pl.BlockSpec(memory_space=pltpu.HBM)
     tokens = jax.ShapeDtypeStruct((T, DH), BF)
-    qo, ko, vo, own = pl.pallas_call(
+    fr, dr = Layout(FH, Z).r, Layout(DH, Z).r
+    columns = jax.ShapeDtypeStruct((NS, LANE), F32)
+    shapes = (tokens, tokens, tokens, jax.ShapeDtypeStruct((dr, FH), F32), columns, columns)
+    results = pl.pallas_call(
         kernel,
-        out_shape=(tokens, tokens, tokens, jax.ShapeDtypeStruct((3, NS, LANE), F32)),
-        in_specs=[anywhere] * len(INPUTS),
-        out_specs=(anywhere,) * 4,
+        out_shape=shapes,
+        in_specs=[hbm] * len(INPUTS),
+        out_specs=(anywhere,) * 6,
         scratch_shapes=scratch.specs,
         compiler_params=pltpu.CompilerParams(
             collective_id=0, has_side_effects=True, vmem_limit_bytes=VMEM_LIMIT
         ),
         name="lact_backward",
-    )(*(arrays[name] for name in INPUTS))
-    fr, dr = Layout(FH, Z).r, Layout(DH, Z).r
-    down = own[0].reshape(FH // LANE, dr, LANE).transpose(0, 2, 1).reshape(CORES, XS, fr, Z, dr)
-    down = down.transpose(3, 1, 0, 2, 4).reshape(1, FH, dr)
-    gate = own[1].reshape(DH // LANE, fr, LANE).transpose(0, 2, 1).reshape(1, DH, fr)
-    up = own[2].reshape(DH // LANE, fr, LANE).transpose(0, 2, 1).reshape(1, DH, fr)
+    )(*(pltpu.with_memory_space_constraint(arrays[name], pltpu.HBM) for name in INPUTS))
+
+    def hand_on(*refs):
+        sems = refs[12]
+        copies = [pltpu.make_async_copy(refs[i], refs[6 + i], sems.at[i]) for i in range(6)]
+        for copy in copies:
+            copy.start()
+        for copy in copies:
+            copy.wait()
+
+    qo, ko, vo, down, gate, up = pl.pallas_call(
+        hand_on,
+        out_shape=shapes,
+        in_specs=[anywhere] * 6,
+        out_specs=(hbm,) * 6,
+        scratch_shapes=[pltpu.SemaphoreType.DMA((6,))],
+        compiler_params=pltpu.CompilerParams(vmem_limit_bytes=1024 * 1024),
+        name="hand_on",
+    )(*results)
+    down = down.T.reshape(1, FH, dr)
+    gate = gate.reshape(DH // LANE, fr, LANE).transpose(0, 2, 1).reshape(1, DH, fr)
+    up = up.reshape(DH // LANE, fr, LANE).transpose(0, 2, 1).reshape(1, DH, fr)
     return qo, ko, vo, gate, up, down
 
 

time: 97.2 us -> 92.5 us (0.952)
  local copies, waits for them, and re-layouts: 5.1 us -> 0 us
    unnamed x10 -> x0, local copies, waits for them, and re-layouts: 3.47 us -> none
    slice x1 -> x0, local copies, waits for them, and re-layouts: 1.33 us -> none  [per_device(): own[0].reshape(FH // LANE, dr, LANE).transpose(0, 2, 1)]
    pallas_call x1 -> x2, Pallas kernels: 91.2 us -> 91.7 us  [the longest x1 90.7 us: per_device(): pl.pallas_call(kernel, out_shape=shapes, in_specs=[hbm] * len(INPUTS), ou...]
where the time goes in v3:
time: 92.5 us; the launch traced here: 92.3 us
  Pallas kernels  91.7 us (99%)
    pallas_call x1, Pallas kernels, per_device(): pl.pallas_call(kernel, out_shape=shapes, in_specs=[hbm] * len(INPUTS), ou...  90.7 us

profile of v3, /device:TPU:1, one launch (start us, length us, event | category | flops | bytes accessed | tf_op | source)
XLA Modules:
  0.0 92.3 jit_solution(12775659691825324107)
XLA Ops:
  0.6 90.7 %lact_backward.1 = (bf16[256,512]{1,0:T(8,128)(2,1)S(1)}, bf16[256,512]{1,0:T(8,128)(2,1)S(1)}, bf16[256,512]{1,0:T(8,128)(2,1)S(1)}, f32[4,256]{1,0:T(4,128)S(1...) custom-call(bf16[512,256]{1,0:T(8,128)(2,1)} %bitcast.18, bf16[512,256]{1,0:T(8,128)(2,1)} %bitcast.19, ...), custom_call_target="tpu_custom_call" | custom-call | tf_op jit(solution)/shard_map/lact_backward/pallas_call | solution.py:648
  91.4 0.9 %hand_on.1 = (bf16[256,512]{1,0:T(8,128)(2,1)}, bf16[256,512]{1,0:T(8,128)(2,1)}, bf16[256,512]{1,0:T(8,128)(2,1)}, f32[4,256]{1,0:T(4,128)}, f32[8,128]{1,0:T(8,128)}, /*index=5*/f32[8,128]{1,0:T(8,128)}) custom-call(bf16[256,512]{1,0:T(8,128)(2,1)S(1)} %get-tuple-element.18.refs_0_, bf16[256,512]{1,0:T(8,128)(2,1)S(1)} %get-tuple-element.19.refs_1_, ...), custom_call_target="tpu_custom_call" | custom-call | tf_op jit(solution)/shard_map/hand_on/pallas_call | solution.py:668

commit v4 on v3

--- a/solution.py
+++ b/solution.py
@@ -13,7 +13,8 @@
 F32 = jnp.float32
 MESH = pl.DeviceIdType.MESH
 VMEM_LIMIT = 24 * 1024 * 1024
-PIECES = ((0,), (1,), (2,))
+QUADS = 4
+MATS = 3
 
 
 def nn(a, b):
@@ -37,14 +38,25 @@
         self.n, self.zs = n, zs
         self.r = n // (CORES * XS * zs)
         self.rows = self.r * zs
+        self.quad = self.rows // QUADS
 
     def natural(self, pos):
-        lz, lr, lx, lc = log2(self.zs), log2(self.r), log2(XS), log2(CORES)
-        z = pos & (self.zs - 1)
-        r = lax.shift_right_logical(pos, lz) & (self.r - 1)
-        x = lax.shift_right_logical(pos, lz + lr) & (XS - 1)
-        c = lax.shift_right_logical(pos, lz + lr + lx) & (CORES - 1)
+        lq, ll, lr, lx, lc = log2(QUADS), log2(self.zs // QUADS), log2(self.r), log2(XS), log2(CORES)
+        low = pos & (self.zs // QUADS - 1)
+        r = lax.shift_right_logical(pos, ll) & (self.r - 1)
+        q = lax.shift_right_logical(pos, ll + lr) & (QUADS - 1)
+        x = lax.shift_right_logical(pos, ll + lr + lq) & (XS - 1)
+        c = lax.shift_right_logical(pos, ll + lr + lq + lx) & (CORES - 1)
+        z = (q << ll) | low
         return (z << (lx + lc + lr)) | (x << (lc + lr)) | (c << lr) | r
+
+    def chunk_row(self, row, per_owner):
+        lq, ll, lr = log2(QUADS), log2(self.zs // QUADS), log2(self.r)
+        low = row & (self.zs // QUADS - 1)
+        r = lax.shift_right_logical(row, ll) & (self.r - 1)
+        q = lax.shift_right_logical(row, ll + lr) & (QUADS - 1)
+        j = lax.shift_right_logical(row, ll + lr + lq)
+        return (((q << ll) | low) << log2(per_owner)) | (j << lr) | r
 
     def onehot(self):
         shape = (self.n, self.n)
@@ -77,6 +89,13 @@
     c = lax.rem(t, CORES)
     x = lax.rem(t // CORES, XS)
     z = t // (CORES * XS)
+    ZL = Z // QUADS
+    QR = BR // QUADS
+    q, zl = z // ZL, lax.rem(z, ZL)
+    quad_order = sorted(range(QUADS), key=lambda k: (-min(k, QUADS - k), k))
+
+    def quad(k):
+        return lax.rem(q + k, QUADS)
 
     def at(c_, x_, z_):
         return (h, (z_ * XS + x_) * CORES + c_)
@@ -91,10 +110,6 @@
 
     def head_peer(k):
         return lax.rem(h + k, heads)
-
-    def z_step(i):
-        half = (i + 1) // 2
-        return Z // 2 + jnp.where(lax.rem(i, 2) == 0, half, -half)
 
     x_order = sorted(range(1, XS), key=lambda k: -min(k, XS - k))
 
@@ -104,18 +119,18 @@
 
     barrier = pltpu.get_barrier_semaphore()
     near = [other] + [at(c, x_peer(k), z) for k in range(1, XS)]
-    near += [at(c, x, z_peer(1)), at(c, x, z_peer(Z - 1))]
+    near += [at(c, x, z_peer(k)) for k in (1, Z - 1, 2, Z - 2)]
     near += [(head_peer(k), t) for k in range(1, heads)]
     for device in near:
         pl.semaphore_signal(barrier, inc=1, device_id=device, device_id_type=MESH)
     for name in INPUTS:
         loads[name].start()
 
-    rounds = log2(Z) - 1
+    rounds = log2(Z) - 2
 
     def reach_signal(i):
         if i < rounds:
-            for k in (2**i, Z - 2**i):
+            for k in (2 * 2**i, Z - 2 * 2**i):
                 pl.semaphore_signal(s.reach.at[i], inc=1, device_id=at(c, x, z_peer(k)), device_id_type=MESH)
 
     def reach_wait(i):
@@ -147,104 +162,119 @@
         return sg, hidden * sg, sg * (1.0 + hidden * (1.0 - sg))
 
     def put(ph, m, val):
-        pc, mi = s.place[m]
         lay, js = layouts[m], JS[m]
-        ref = s.sb[ph][pc]
         for cx in range(CORES * XS):
-            for j in range(js):
-                lo = mi * BR + j * lay.rows
-                ref[cx // XS, cx % XS, lo:lo + lay.rows, :] = val[
-                    cx * lay.rows:(cx + 1) * lay.rows, j * LANE:(j + 1) * LANE
-                ].astype(BF)
-
-    def rs_core(ph, pc):
-        remote(s.sb[ph][pc].at[1 - c], s.cr[ph][pc], s.sems.at[ph, pc, 0], s.sems.at[ph, pc, 1], other).start()
-
-    def rs_x(ph, pc):
-        sb, cr, xs, xr = s.sb[ph][pc], s.cr[ph][pc], s.xs[ph][pc], s.xr[ph][pc]
-        remote(sb.at[1 - c], cr, s.sems.at[ph, pc, 0], s.sems.at[ph, pc, 1], other).wait_recv()
-        for k in x_order:
-            xd = x_peer(k)
-            xs[xd] = (sb[c, xd].astype(F32) + cr[xd].astype(F32)).astype(BF)
+            for qq in range(QUADS):
+                row = cx * lay.rows + qq * lay.quad
+                for j in range(js):
+                    lo = m * QR + j * lay.quad
+                    s.sb[ph][cx // XS, qq, cx % XS, lo:lo + lay.quad, :] = val[
+                        row:row + lay.quad, j * LANE:(j + 1) * LANE
+                    ].astype(BF)
+
+    def core_copy(ph, k):
+        qq = quad(k)
+        return remote(s.sb[ph].at[1 - c, qq], s.cr[ph].at[qq], s.sems.at[ph, 0, k], s.sems.at[ph, 1, k], other)
+
+    def rs_core(ph):
+        for k in quad_order:
+            core_copy(ph, k).start()
+
+    def rs_x(ph, k):
+        qq = quad(k)
+        sb, cr, xs, xr = s.sb[ph], s.cr[ph], s.xs[ph], s.xr[ph]
+        core_copy(ph, k).wait_recv()
+        for i in x_order:
+            xd = x_peer(i)
+            xs[qq, xd] = (sb[c, qq, xd].astype(F32) + cr[qq, xd].astype(F32)).astype(BF)
             remote(
-                xs.at[xd], xr.at[x], s.sems.at[ph, pc, 2], s.sems.at[ph, pc, 3], at(c, xd, z)
+                xs.at[qq, xd], xr.at[k, x], s.sems.at[ph, 2, k], s.sems.at[ph, 3, k], at(c, xd, z)
             ).start()
-        s.acc[pc][...] = sb[c, x].astype(F32) + cr[x].astype(F32)
-
-    def rs_z(ph, pc):
-        xr, zs, zr = s.xr[ph][pc], s.zs[ph][pc], s.zr[ph][pc]
-        span = xr.at[pl.ds(0, XS - 1)]
-        remote(span, span, s.sems.at[ph, pc, 2], s.sems.at[ph, pc, 3], other).wait_recv()
-        total = s.acc[pc][...]
-        for k in range(1, XS):
-            total = total + xr[x_peer(k)].astype(F32)
-        total = total.astype(BF)
-        for mi in range(len(PIECES[pc])):
-            chunks = nn(s.perm[...], total[mi * BR:(mi + 1) * BR])
-            zs[:, mi * NS:(mi + 1) * NS, :] = chunks.reshape(Z, NS, LANE).astype(BF)
-
-        def send(i, carry):
-            zd = z_peer(z_step(i))
+        s.acc[qq] = sb[c, qq, x].astype(F32) + cr[qq, x].astype(F32)
+
+    def three(ref, ph, k):
+        span = ref.at[k, pl.ds(0, XS - 1)]
+        return remote(span, span, s.sems.at[ph, 2, k], s.sems.at[ph, 3, k], other)
+
+    def rs_z(ph, k):
+        qq = quad(k)
+        xr, zs, zr = s.xr[ph], s.zs[ph], s.zr[ph]
+        three(xr, ph, k).wait_recv()
+        total = s.acc[qq]
+        for i in range(1, XS):
+            total = total + xr[k, x_peer(i)].astype(F32)
+        total = jnp.concatenate([total[m * QR:(m + 1) * QR] for m in range(MATS)], axis=1).astype(BF)
+        chunks = nn(s.perm[...], total)
+        for m in range(MATS):
+            zs[qq, :, m * NS:(m + 1) * NS, :] = chunks[:, m * LANE:(m + 1) * LANE].reshape(ZL, NS, LANE).astype(BF)
+        for i in range(1, ZL) if k == 0 else range(ZL):
+            ll = lax.rem(zl + i, ZL)
             remote(
-                zs.at[zd], zr.at[z], s.sems.at[ph, pc, 4], s.sems.at[ph, pc, 5], at(c, x, zd)
+                zs.at[qq, ll], zr.at[z], s.sems.at[ph, 4, 0], s.sems.at[ph, 5, 0], at(c, x, qq * ZL + ll)
             ).start()
-            return carry
-
-        lax.fori_loop(0, Z - 1, send, 0)
-
-    def rs_own(ph, pc):
-        zs, zr = s.zs[ph][pc], s.zr[ph][pc]
-        span = zr.at[pl.ds(0, Z - 1)]
-        remote(span, span, s.sems.at[ph, pc, 4], s.sems.at[ph, pc, 5], other).wait_recv()
-        total = zs[z].astype(F32)
+
+    def rs_z_all(ph):
+        span = s.zr[ph].at[pl.ds(0, Z - 1)]
+        return remote(span, span, s.sems.at[ph, 4, 0], s.sems.at[ph, 5, 0], other)
+
+    def rs_own(ph):
+        rs_z_all(ph).wait_recv()
+        total = s.zs[ph][q, zl].astype(F32)
         for k in range(1, Z):
-            total = total + zr[z_peer(k)].astype(F32)
-        return [total[mi * NS:(mi + 1) * NS] for mi in range(len(PIECES[pc]))]
+            total = total + s.zr[ph][z_peer(k)].astype(F32)
+        return [total[m * NS:(m + 1) * NS] for m in range(MATS)]
 
     def rs_drain(ph):
-        for pc in range(len(PIECES)):
-            sb, xr, zr = s.sb[ph][pc], s.xr[ph][pc], s.zr[ph][pc]
-            for i, span in ((0, sb.at[1 - c]), (2, xr.at[pl.ds(0, XS - 1)]), (4, zr.at[pl.ds(0, Z - 1)])):
-                remote(span, span, s.sems.at[ph, pc, i], s.sems.at[ph, pc, i + 1], other).wait_send()
-
-    def ag_z(ph, pc, vals):
-        ab, base = s.ab[ph][pc], 3 + ph
-        for mi, val in enumerate(vals):
-            ab[c, x, z, mi * NS:(mi + 1) * NS, :] = val.astype(BF)
-
-        def send(i, carry):
-            zd = z_peer(z_step(i))
-            mine = ab.at[c, x, z]
-            remote(mine, mine, s.sems.at[base, pc, 4], s.sems.at[base, pc, 5], at(c, x, zd)).start()
-            return carry
-
-        lax.fori_loop(0, Z - 1, send, 0)
-
-    def ag_x(ph, pc):
-        ab, base = s.ab[ph][pc], 3 + ph
-        span = ab.at[c, x, pl.ds(0, Z - 1)]
-        remote(span, span, s.sems.at[base, pc, 4], s.sems.at[base, pc, 5], other).wait_recv()
-        mine = ab.at[c, x]
-        for k in x_order:
+        for k in quad_order:
+            core_copy(ph, k).wait_send()
+            three(s.xr[ph], ph, k).wait_send()
+        rs_z_all(ph).wait_send()
+
+    def ag_z(ph, vals):
+        ab, base = s.ab[ph], 3 + ph
+        ab[c, q, x, zl] = jnp.concatenate(vals, axis=0).astype(BF)
+        mine = ab.at[c, q, x, zl]
+        for k in quad_order:
+            for i in range(1, ZL) if k == 0 else range(ZL):
+                ll = lax.rem(zl + i, ZL)
+                remote(
+                    mine, mine, s.sems.at[base, 4, k], s.sems.at[base, 5, (QUADS - k) % QUADS],
+                    at(c, x, quad(k) * ZL + ll),
+                ).start()
+
+    def ag_z_quad(ph, k):
+        n = ZL - 1 if k == 0 else ZL
+        span = s.ab[ph].at[c, quad(k), x, pl.ds(0, n)]
+        return remote(span, span, s.sems.at[3 + ph, 4, k], s.sems.at[3 + ph, 5, k], other)
+
+    def ag_x(ph, k):
+        base = 3 + ph
+        ag_z_quad(ph, k).wait_recv()
+        mine = s.ab[ph].at[c, quad(k), x]
+        for i in x_order:
             remote(
-                mine, mine, s.sems.at[base, pc, 2], s.sems.at[base, pc, 3], at(c, x_peer(k), z)
+                mine, mine, s.sems.at[base, 2, k], s.sems.at[base, 3, k], at(c, x_peer(i), z)
             ).start()
 
-    def ag_core(ph, pc):
-        ab, base = s.ab[ph][pc], 3 + ph
-        span = ab.at[c, pl.ds(0, XS - 1)]
-        remote(span, span, s.sems.at[base, pc, 2], s.sems.at[base, pc, 3], other).wait_recv()
-        mine = ab.at[c]
-        remote(mine, mine, s.sems.at[base, pc, 0], s.sems.at[base, pc, 1], other).start()
-
-    def unpack(ph, pc, cc, dst):
-        ab = s.ab[ph][pc]
-        for mi, m in enumerate(PIECES[pc]):
+    def ag_x_quad(ph, k):
+        span = s.ab[ph].at[c, quad(k), pl.ds(0, XS - 1)]
+        return remote(span, span, s.sems.at[3 + ph, 2, k], s.sems.at[3 + ph, 3, k], other)
+
+    def ag_core_quad(ph, k, cc):
+        span = s.ab[ph].at[cc, quad(k)]
+        return remote(span, span, s.sems.at[3 + ph, 0, k], s.sems.at[3 + ph, 1, k], other)
+
+    def unpack(ph, cc, dst):
+        for m in range(MATS):
             lay, js = layouts[m], JS[m]
             blocks = jnp.concatenate(
-                [ab[cc, xx, :, mi * NS:(mi + 1) * NS, :].astype(F32).reshape(BR, LANE) for xx in range(XS)], axis=1
+                [
+                    s.ab[ph][cc, :, xx, :, m * NS:(m + 1) * NS, :].astype(F32).reshape(BR, LANE)
+                    for xx in range(XS)
+                ],
+                axis=1,
             )
-            rows = nn(s.permt[...], blocks.astype(BF)).astype(BF)
+            rows = nn((s.permd if m == 0 else s.permf)[...], blocks.astype(BF)).astype(BF)
             for xx in range(XS):
                 lo = pl.multiple_of((cc * XS + xx) * lay.rows, lay.rows)
                 for j in range(js):
@@ -252,21 +282,26 @@
                         j * lay.rows:(j + 1) * lay.rows, xx * LANE:(xx + 1) * LANE
                     ]
 
-    def ag_finish(ph, dst):
-        for pc in range(len(PIECES)):
-            unpack(ph, pc, c, dst)
-        for pc in range(len(PIECES)):
-            ab, base = s.ab[ph][pc], 3 + ph
-            theirs = ab.at[1 - c]
-            remote(theirs, theirs, s.sems.at[base, pc, 0], s.sems.at[base, pc, 1], other).wait_recv()
-            unpack(ph, pc, 1 - c, dst)
+    def gather(ph, vals, dst):
+        ag_z(ph, vals)
+        arrival = sorted(range(QUADS), key=lambda k: (min(k, QUADS - k), k))
+        for k in arrival:
+            ag_x(ph, k)
+        for k in arrival:
+            ag_x_quad(ph, k).wait_recv()
+            ag_core_quad(ph, k, c).start()
+        unpack(ph, c, dst)
+        for k in arrival:
+            ag_core_quad(ph, k, 1 - c).wait_recv()
+        unpack(ph, 1 - c, dst)
 
     def ag_drain(ph):
-        base = 3 + ph
-        for pc in range(len(PIECES)):
-            ab = s.ab[ph][pc]
-            for i, span in ((0, ab.at[c]), (2, ab.at[c, pl.ds(0, XS - 1)]), (4, ab.at[c, x, pl.ds(0, Z - 1)])):
-                remote(span, span, s.sems.at[base, pc, i], s.sems.at[base, pc, i + 1], other).wait_send()
+        for k in quad_order:
+            n = ZL - 1 if k == 0 else ZL
+            span = s.ab[ph].at[c, q, x, pl.ds(0, n)]
+            remote(span, span, s.sems.at[3 + ph, 4, k], s.sems.at[3 + ph, 5, k], other).wait_send()
+            ag_x_quad(ph, k).wait_send()
+            ag_core_quad(ph, k, c).wait_send()
 
     def colsum(val, r):
         total = jnp.broadcast_to(jnp.sum(val, axis=1, keepdims=True), (NS, LANE))
@@ -275,8 +310,6 @@
             total = total + pltpu.roll(total, shift, 0)
             shift *= 2
         return total
-
-    pieces = range(len(PIECES))
 
     def put_down(val):
         high = val.astype(BF).astype(F32)
@@ -291,15 +324,18 @@
             total = part if total is None else total + part
         s.own0[...] = total
 
+    def match(left, right):
+        return jnp.where(left == right, 1.0, 0.0).astype(BF)
+
+    small = (QR, QR)
+    rows_i, cols_i = lax.broadcasted_iota(jnp.int32, small, 0), lax.broadcasted_iota(jnp.int32, small, 1)
+    s.perm[...] = match(
+        rows_i, ((cols_i & (ZL - 1)) << log2(NS)) | lax.shift_right_logical(cols_i, log2(ZL))
+    )
     rows_i = lax.broadcasted_iota(jnp.int32, (BR, BR), 0)
     cols_i = lax.broadcasted_iota(jnp.int32, (BR, BR), 1)
-    lz, ln = log2(Z), log2(NS)
-    s.perm[...] = jnp.where(
-        cols_i == (((rows_i & (NS - 1)) << lz) | lax.shift_right_logical(rows_i, ln)), 1.0, 0.0
-    ).astype(BF)
-    s.permt[...] = jnp.where(
-        rows_i == (((cols_i & (NS - 1)) << lz) | lax.shift_right_logical(cols_i, ln)), 1.0, 0.0
-    ).astype(BF)
+    s.permd[...] = match(dl.chunk_row(rows_i, NS), cols_i)
+    s.permf[...] = match(fl.chunk_row(rows_i, NS), cols_i)
     s.pft[...] = fl.onehot_t()
     w1t, w3t, w2t = s.w1t, s.w3t, s.w2t
     s.pd[...] = dl.onehot()
@@ -327,9 +363,6 @@
     each_rows(scale_v)
     s.vp[...] = nn(s.vn[...], s.pd[...]).astype(BF)
     put(0, 0, tn(s.vp[...], s.mixed[...]))
-    pl.semaphore_wait(barrier, len(near))
-    reach_signal(0)
-    rs_core(0, 0)
     loads["w2"].wait()
     w2t[...] = tn(nn(w2_ref[...], s.pd[...]).astype(BF), fl.onehot()).astype(BF)
     s.db[...] = nn(s.vp[...], w2t[...])
@@ -342,21 +375,20 @@
 
     each_rows(backs)
     put(0, 1, tn(s.gb[...], k_ref[...]))
-    rs_core(0, 1)
+    pl.semaphore_wait(barrier, len(near))
+    reach_signal(0)
     put(0, 2, tn(s.ub[...], k_ref[...]))
-    rs_core(0, 2)
-    reach_wait(0)
-    reach_signal(1)
-    rs_x(0, 0)
-    rs_x(0, 1)
-    reach_wait(1)
-    reach_signal(2)
-    rs_x(0, 2)
-    for i in range(2, rounds):
+    rs_core(0)
+    for i, k in enumerate(quad_order):
+        rs_x(0, k)
+        if i == 0:
+            reach_wait(0)
+            reach_signal(1)
+    for i in range(1, rounds):
         reach_wait(i)
         reach_signal(i + 1)
-    for pc in pieces:
-        rs_z(0, pc)
+    for k in quad_order:
+        rs_z(0, k)
 
     priors = [None] * 3
     for m, wt in ((0, w2t), (1, w1t), (2, w3t)):
@@ -365,7 +397,7 @@
         block = jnp.concatenate(
             [wt[pl.ds(lo, lay.rows), j * LANE:(j + 1) * LANE] for j in range(js)], axis=0
         )
-        s.prior[...] = nn(s.perm[...], block)
+        s.prior[...] = tn((s.permd if m == 0 else s.permf)[...], block)
         priors[m] = s.prior[pl.ds(pl.multiple_of(z * NS, NS), NS), :]
     loads["gain_row"].wait()
     loads["g"].wait()
@@ -379,24 +411,17 @@
     gain_p = jnp.sum(nn(split.astype(BF), s.pd[...]), axis=0, keepdims=True)
     s.gw[...] = nn(g_ref[...], s.pd[...]) * gain_p
 
-    sums = [None] * 3
     moved, prior_norm, moved_norm = [None] * 3, [None] * 3, [None] * 3
     for m in range(3):
         prior_norm[m] = jnp.sqrt(colsum(priors[m] * priors[m], layouts[m].r) + EPSILON)
-    for pc in pieces:
-        got = rs_own(0, pc)
-        fast = []
-        for mi, m in enumerate(PIECES[pc]):
-            moved[m] = priors[m] - got[mi]
-            moved_norm[m] = jnp.sqrt(colsum(moved[m] * moved[m], layouts[m].r) + EPSILON)
-            fast.append(moved[m] * (prior_norm[m] / moved_norm[m]))
-        ag_z(0, pc, fast)
-    for pc in pieces:
-        ag_x(0, pc)
-    for pc in pieces:
-        ag_core(0, pc)
+    got = rs_own(0)
+    fast = []
+    for m in range(MATS):
+        moved[m] = priors[m] - got[m]
+        moved_norm[m] = jnp.sqrt(colsum(moved[m] * moved[m], layouts[m].r) + EPSILON)
+        fast.append(moved[m] * (prior_norm[m] / moved_norm[m]))
     f1t, f3t, f2t = s.f1t, s.f3t, s.f2t
-    ag_finish(0, (f2t, f1t, f3t))
+    gather(0, fast, (f2t, f1t, f3t))
 
     s.qg[...] = nt(q_ref[...], f1t[...])
     s.qu[...] = nt(q_ref[...], f3t[...])
@@ -440,7 +465,6 @@
     each_rows(outback)
 
     put(1, 0, tn(s.ob[...], s.qm[...]))
-    rs_core(1, 0)
     s.qb[...] = nn(s.ob[...], f2t[...])
 
     def qbacks(rows):
@@ -451,34 +475,27 @@
 
     each_rows(qbacks)
     put(1, 1, tn(s.qgb[...], q_ref[...]))
-    rs_core(1, 1)
     put(1, 2, tn(s.qub[...], q_ref[...]))
-    rs_core(1, 2)
-    for pc in pieces:
-        rs_x(1, pc)
-    for pc in pieces:
-        rs_z(1, pc)
+    rs_core(1)
+    for k in quad_order:
+        rs_x(1, k)
+    for k in quad_order:
+        rs_z(1, k)
     s.qo[...] = (nn(s.qgb[...], f1t[...]) + nn(s.qub[...], f3t[...])).astype(BF)
     stores = [pltpu.make_async_copy(s.qo, outs[0], s.outsem.at[0])]
     stores[0].start()
 
     owned = [None] * 3
-    for pc in pieces:
-        got = rs_own(1, pc)
-        cot = []
-        for mi, m in enumerate(PIECES[pc]):
-            grad, mn, pn = got[mi], moved_norm[m], prior_norm[m]
-            dot = colsum(grad * moved[m], layouts[m].r)
-            moved_grad = pn / mn * (grad - moved[m] * (dot / (mn * mn)))
-            owned[m] = moved_grad + priors[m] * (dot / (mn * pn))
-            cot.append(moved_grad)
-        ag_z(1, pc, cot)
-    for pc in pieces:
-        ag_x(1, pc)
-    for pc in pieces:
-        ag_core(1, pc)
+    got = rs_own(1)
+    cot = []
+    for m in range(MATS):
+        grad, mn, pn = got[m], moved_norm[m], prior_norm[m]
+        dot = colsum(grad * moved[m], layouts[m].r)
+        moved_grad = pn / mn * (grad - moved[m] * (dot / (mn * mn)))
+        owned[m] = moved_grad + priors[m] * (dot / (mn * pn))
+        cot.append(moved_grad)
     c1t, c3t, c2t = s.c1t, s.c3t, s.c2t
-    ag_finish(1, (c2t, c1t, c3t))
+    gather(1, cot, (c2t, c1t, c3t))
 
     s.qg[...] = nt(k_ref[...], c1t[...])
     s.qu[...] = nt(k_ref[...], c3t[...])
@@ -495,15 +512,13 @@
 
     each_rows(bars)
     put(2, 0, tn(s.vp[...], s.dbb[...]))
-    rs_core(2, 0)
     put(2, 1, tn(s.qgb[...], k_ref[...]))
-    rs_core(2, 1)
     put(2, 2, tn(s.qub[...], k_ref[...]))
-    rs_core(2, 2)
-    for pc in pieces:
-        rs_x(2, pc)
-    for pc in pieces:
-        rs_z(2, pc)
+    rs_core(2)
+    for k in quad_order:
+        rs_x(2, k)
+    for k in quad_order:
+        rs_z(2, k)
 
     s.out[...] = nt(s.mixed[...], c2t[...]) + nt(s.dbb[...], w2t[...])
 
@@ -520,18 +535,17 @@
     stores.append(pltpu.make_async_copy(s.ko, outs[1], s.outsem.at[2]))
     stores[2].start()
 
-    for pc in pieces:
-        got = rs_own(2, pc)
-        for mi, m in enumerate(PIECES[pc]):
-            final = owned[m] - got[mi]
-            if m == 0:
-                put_down(final)
-                stores.append(pltpu.make_async_copy(s.own0, outs[3], s.outsem.at[3]))
-            else:
-                own = (s.own1, s.own2)[m - 1]
-                own[...] = final
-                stores.append(pltpu.make_async_copy(own, outs[3 + m], s.outsem.at[3 + m]))
-            stores[-1].start()
+    got = rs_own(2)
+    for m in range(MATS):
+        final = owned[m] - got[m]
+        if m == 0:
+            put_down(final)
+            stores.append(pltpu.make_async_copy(s.own0, outs[3], s.outsem.at[3]))
+        else:
+            own = (s.own1, s.own2)[m - 1]
+            own[...] = final
+            stores.append(pltpu.make_async_copy(own, outs[3 + m], s.outsem.at[3 + m]))
+        stores[-1].start()
     for ph in range(3):
         rs_drain(ph)
     for ph in range(2):
@@ -579,29 +593,29 @@
         vm("own2", NS, LANE, dtype=F32)
         vm("pft", FH, FH)
         vm("pd", DH, DH)
-        vm("perm", BR, BR)
-        vm("permt", BR, BR)
+        QR, ZL = BR // QUADS, Z // QUADS
+        vm("perm", QR, QR)
+        vm("permd", BR, BR)
+        vm("permf", BR, BR)
         vm("prior", BR, LANE, dtype=F32)
         vm("hs", 8, T, dtype=F32)
         vm("hr", heads, 8, T, dtype=F32)
-        for pc, ms in enumerate(PIECES):
-            n = len(ms)
-            vm(("acc", pc), n * BR, LANE, dtype=F32)
-            for ph in range(3):
-                vm(("sb", ph, pc), CORES, XS, n * BR, LANE)
-                vm(("cr", ph, pc), XS, n * BR, LANE)
-                vm(("xs", ph, pc), XS, n * BR, LANE)
-                vm(("xr", ph, pc), XS, n * BR, LANE)
-                vm(("zs", ph, pc), Z, n * NS, LANE)
-                vm(("zr", ph, pc), Z, n * NS, LANE)
-            for ph in range(2):
-                vm(("ab", ph, pc), CORES, XS, Z, n * NS, LANE)
+        vm("acc", QUADS, MATS * QR, LANE, dtype=F32)
+        for ph in range(3):
+            vm(("sb", ph), CORES, QUADS, XS, MATS * QR, LANE)
+            vm(("cr", ph), QUADS, XS, MATS * QR, LANE)
+            vm(("xs", ph), QUADS, XS, MATS * QR, LANE)
+            vm(("xr", ph), QUADS, XS, MATS * QR, LANE)
+            vm(("zs", ph), QUADS, ZL, MATS * NS, LANE)
+            vm(("zr", ph), Z, MATS * NS, LANE)
+        for ph in range(2):
+            vm(("ab", ph), CORES, QUADS, XS, ZL, MATS * NS, LANE)
         for name, shape in (
-            ("sems", (5, len(PIECES), 6)), ("hsem", (2,)), ("insem", (len(INPUTS),)), ("outsem", (6,))
+            ("sems", (5, 6, QUADS)), ("hsem", (2,)), ("insem", (len(INPUTS),)), ("outsem", (6,))
         ):
             self.specs.append(pltpu.SemaphoreType.DMA(shape))
             self.names.append(name)
-        self.specs.append(pltpu.SemaphoreType.REGULAR((max(1, log2(Z) - 1),)))
+        self.specs.append(pltpu.SemaphoreType.REGULAR((max(1, log2(Z) - 2),)))
         self.names.append("reach")
 
     def bind(self, refs):
@@ -609,18 +623,13 @@
             pass
 
         s = Refs()
-        s.place = {m: (pc, mi) for pc, ms in enumerate(PIECES) for mi, m in enumerate(ms)}
-        for name in ("sb", "cr", "xs", "xr", "zs", "zr"):
-            setattr(s, name, [[None] * len(PIECES) for _ in range(3)])
-        s.ab = [[None] * len(PIECES) for _ in range(2)]
-        s.acc = [None] * len(PIECES)
         for name, ref in zip(self.names, refs):
             if isinstance(name, str):
                 setattr(s, name, ref)
-            elif len(name) == 2:
-                s.acc[name[1]] = ref
             else:
-                getattr(s, name[0])[name[1]][name[2]] = ref
+                held = getattr(s, name[0], [])
+                held.append(ref)
+                setattr(s, name[0], held)
         return s
 
 

time: 92.5 us -> 90.9 us (0.983)
  Pallas kernels: 91.7 us -> 89.6 us
    pallas_call x1, Pallas kernels: 90.7 us -> 88.6 us  [per_device(): pl.pallas_call(kernel, out_shape=shapes, in_specs=[hbm] * len(INPUTS), ou...]
where the time goes in v4:
time: 90.9 us; the launch traced here: 90.2 us
  Pallas kernels  89.6 us (99%)
    pallas_call x1, Pallas kernels, per_device(): pl.pallas_call(kernel, out_shape=shapes, in_specs=[hbm] * len(INPUTS), ou...  88.6 us

profile of v4, /device:TPU:1, one launch (start us, length us, event | category | flops | bytes accessed | tf_op | source)
XLA Modules:
  0.0 90.2 jit_solution(4161127745429991292)
XLA Ops:
  0.6 88.6 %lact_backward.1 = (bf16[256,512]{1,0:T(8,128)(2,1)S(1)}, bf16[256,512]{1,0:T(8,128)(2,1)S(1)}, bf16[256,512]{1,0:T(8,128)(2,1)S(1)}, f32[4,256]{1,0:T(4,128)S(1...) custom-call(bf16[512,256]{1,0:T(8,128)(2,1)} %bitcast.18, bf16[512,256]{1,0:T(8,128)(2,1)} %bitcast.19, ...), custom_call_target="tpu_custom_call" | custom-call | tf_op jit(solution)/shard_map/lact_backward/pallas_call | solution.py:657
  89.3 0.9 %hand_on.1 = (bf16[256,512]{1,0:T(8,128)(2,1)}, bf16[256,512]{1,0:T(8,128)(2,1)}, bf16[256,512]{1,0:T(8,128)(2,1)}, f32[4,256]{1,0:T(4,128)}, f32[8,128]{1,0:T(8,128)}, /*index=5*/f32[8,128]{1,0:T(8,128)}) custom-call(bf16[256,512]{1,0:T(8,128)(2,1)S(1)} %get-tuple-element.18.refs_0_, bf16[256,512]{1,0:T(8,128)(2,1)S(1)} %get-tuple-element.19.refs_1_, ...), custom_call_target="tpu_custom_call" | custom-call | tf_op jit(solution)/shard_map/hand_on/pallas_call | solution.py:677
